TPU v7x, 32 devices: a whole 2x2x4 slice. The times are simulated.
32 devices in a mesh: ep: 16 (over z, y, x), tp: 2 (over core).
Axes of the slice: x: 2, y: 2, z: 4, core: 2. Of those that a mesh axis runs over, the one named last changes fastest.
Arguments:
- tokens: bfloat16 [4096, 4096], P(('ep', 'tp')), may hold values from -6 to 6
- expert_ids: int32 [4096, 8], P(('ep', 'tp')), may hold values from 0 to 127, as said below
- gate_weights: float32 [4096, 8], P(('ep', 'tp')), may hold values from 0.1 to 1
- grad_out: bfloat16 [4096, 4096], P(('ep', 'tp')), may hold values from -6 to 6
- w_gate: bfloat16 [16, 768, 4096], P('ep', 'tp'), may hold values from -0.09375 to 0.09375
- w_up: bfloat16 [16, 768, 4096], P('ep', 'tp'), may hold values from -0.09375 to 0.09375
- w_down: bfloat16 [16, 768, 4096], P('ep', 'tp'), may hold values from -0.21875 to 0.21875
Outputs:
- grad_tokens: bfloat16 [4096, 4096], P(('ep', 'tp'))
- grad_gate: bfloat16 [16, 768, 4096], P('ep', 'tp')
- grad_up: bfloat16 [16, 768, 4096], P('ep', 'tp')
- grad_down: bfloat16 [16, 768, 4096], P('ep', 'tp')
Inputs may be any that keep to these rules, and one draw needn't show every extreme that they name: `expert_ids`: each token names 8 different experts. No expert below 16 is named by more than 8 tokens of one device's rows, and in every draw some expert below 16 is named by exactly 8 tokens of every device's rows.
All inputs are finite; a program needn't handle non-finite values.
Results may differ from a plain program's by a relative error of at most 0.0064.
Values may be sent and summed in bfloat16 or wider, within the bound.
No kernel may reach another device: no remote copies, remote signals or barrier semaphores. Data moves between devices by JAX's collectives and lax.ppermute only.
A program may use at most 192 MiB of HBM per device.

v0:
```python
import jax
import jax.numpy as jnp
from jax import lax
from jax.sharding import PartitionSpec as P

CAP = 8


def expert_terms(rows_x, rows_dy, gate_rows, up_rows, down_rows):
    contract_last = (((1,), (1,)), ((), ()))
    contract_first = (((0,), (0,)), ((), ()))
    pre_gate = lax.dot_general(rows_x, gate_rows, contract_last, preferred_element_type=jnp.float32)
    pre_up = lax.dot_general(rows_x, up_rows, contract_last, preferred_element_type=jnp.float32)
    sigmoid_gate = jax.nn.sigmoid(pre_gate)
    activated = (pre_gate * sigmoid_gate * pre_up).astype(jnp.bfloat16)
    d_act = lax.dot_general(rows_dy, down_rows, contract_last, preferred_element_type=jnp.float32)
    d_up = (d_act * pre_gate * sigmoid_gate).astype(jnp.bfloat16)
    d_pre = (d_act * pre_up * sigmoid_gate * (1.0 + pre_gate * (1.0 - sigmoid_gate))).astype(
        jnp.bfloat16
    )
    grad_gate = lax.dot_general(d_pre, rows_x, contract_first, preferred_element_type=jnp.float32)
    grad_up = lax.dot_general(d_up, rows_x, contract_first, preferred_element_type=jnp.float32)
    grad_down = lax.dot_general(
        activated, rows_dy, contract_first, preferred_element_type=jnp.float32
    )
    return (grad_gate, grad_up, grad_down, d_pre, d_up)


def local(tokens, expert_ids, gate_weights, grad_out, w_gate, w_up, w_down):
    window = lax.axis_size("ep")
    slots = CAP
    experts_here = jnp.arange(window, dtype=jnp.int32)
    hit = expert_ids[:, :, None] == experts_here[None, None, :]
    member = jnp.sum(hit.astype(jnp.int32), axis=1)
    before = jnp.cumsum(member, axis=0) - member
    position = jnp.sum(jnp.where(hit, before[:, None, :], 0), axis=2)
    in_window = expert_ids < window
    target = jnp.where(in_window, expert_ids * slots + position, -1)
    slot_index = jnp.arange(window * slots, dtype=jnp.int32)
    match = target[None, :, :] == slot_index[:, None, None]
    placing = jnp.any(match, axis=2).astype(jnp.bfloat16)
    slot_gate = jnp.sum(jnp.where(match, gate_weights[None, :, :], 0.0), axis=(1, 2))
    send_x = jnp.dot(placing, tokens, preferred_element_type=jnp.float32).astype(jnp.bfloat16)
    picked_dy = jnp.dot(placing, grad_out, preferred_element_type=jnp.float32)
    send_dy = (slot_gate[:, None] * picked_dy).astype(jnp.bfloat16)
    gate_rows = w_gate[0]
    up_rows = w_up[0]
    down_rows = w_down[0]
    joined = jnp.concatenate([gate_rows, up_rows], axis=0)
    recv_x, recv_dy = (
        lax.all_to_all(send_x, "ep", split_axis=0, concat_axis=0, tiled=True),
        lax.all_to_all(send_dy, "ep", split_axis=0, concat_axis=0, tiled=True),
    )
    grad_gate, grad_up, grad_down, d_pre, d_up = expert_terms(
        lax.all_gather(recv_x, "tp", axis=0, tiled=True),
        lax.all_gather(recv_dy, "tp", axis=0, tiled=True),
        gate_rows,
        up_rows,
        down_rows,
    )
    fold_stored = jnp.concatenate([d_pre, d_up], axis=1)
    summed = lax.psum_scatter(
        jnp.dot(fold_stored, joined, preferred_element_type=jnp.float32),
        "tp",
        scatter_dimension=0,
        tiled=True,
    )
    returned = lax.all_to_all(
        summed.astype(jnp.bfloat16), "ep", split_axis=0, concat_axis=0, tiled=True
    )
    contract_first = (((0,), (0,)), ((), ()))
    grad_tokens = lax.dot_general(
        placing, returned, contract_first, preferred_element_type=jnp.float32
    ).astype(jnp.bfloat16)
    return (
        grad_tokens,
        grad_gate.astype(jnp.bfloat16)[None],
        grad_up.astype(jnp.bfloat16)[None],
        grad_down.astype(jnp.bfloat16)[None],
    )


def solution(mesh):
    in_specs = (
        P(("ep", "tp"), None),
        P(("ep", "tp"), None),
        P(("ep", "tp"), None),
        P(("ep", "tp"), None),
        P("ep", "tp", None),
        P("ep", "tp", None),
        P("ep", "tp", None),
    )
    out_specs = (
        P(("ep", "tp"), None),
        P("ep", "tp", None),
        P("ep", "tp", None),
        P("ep", "tp", None),
    )
    return jax.shard_map(local, mesh=mesh, in_specs=in_specs, out_specs=out_specs, check_vma=False)
```

profile of v0, /device:TPU:8, one launch (start us, length us, event | category | flops | bytes accessed | tf_op | source)
XLA Modules:
  0.0 155.4 jit_solution(2636452571687611746)
XLA Ops:
  7.2 0.0 copy-start
  7.2 0.0 all-gather.3.cloned.1.call-start
  7.2 0.9 convert_reduce_fusion
  8.1 0.1 copy.14
  8.2 0.2 reduce_window_sum.11
  8.4 0.1 copy.16
  8.4 0.7 select_reduce_fusion.1
  9.1 0.7 add_select_fusion
  9.8 0.2 fusion.13
  10.0 1.7 %select_reduce_fusion = f32[128]{0:T(128)S(1)} fusion(f32[128,8]{0,1:T(8,128)} %param.9, s32[128,8]{0,1:T(8,128)S(1)} %add_select_fusion), kind=kLoop, calls=%fused_computation.20 | loop fusion | flops 393088 | bytes 8704 | tf_op jit(solution)/shard_map/reduce_sum | solution.py:42
  11.7 1.6 %fusion.9 = bf16[16,8,4096]{2,1,0:T(8,128)(2,1)S(1)} fusion(pred[128,128]{1,0:T(8,128)(4,1)S(1)} %fusion.13, bf16[128,4096]{1,0:T(8,128)(2,1)} %param.10, f32[128]{0:T(128)S(1)} %select_reduce_fusion), kind=kOutput, calls=%fused_computation.15 | convolution fusion | flops 135266304 | bytes 2114048 | tf_op jit(solution)/shard_map/dot_general | solution.py:44
  13.4 32.8 %all_to_all.36 = bf16[16,8,4096]{2,1,0:T(8,128)(2,1)} all-to-all(bf16[16,8,4096]{2,1,0:T(8,128)(2,1)S(1)} %fusion.9), channel_id=1, replica_groups=mesh['ep'=16,'tp'=2] {'ep'}, dimensions={0} | all-to-all | bytes 2097152 | tf_op jit(solution)/shard_map/all_to_all | solution.py:52
  46.2 0.0 all-gather.3.cloned.1.call-update
  46.3 0.0 all-gather.5.cloned.1.call-start
  46.3 1.7 %fusion.8 = bf16[16,8,4096]{2,1,0:T(8,128)(2,1)S(1)} fusion(pred[128,128]{1,0:T(8,128)(4,1)S(1)} %fusion.13, bf16[128,4096]{1,0:T(8,128)(2,1)} %param.7), kind=kOutput, calls=%fused_computation.14 | convolution fusion | flops 134742016 | bytes 2113536 | tf_op jit(solution)/shard_map/dot_general | solution.py:43
  48.0 29.5 %all_to_all.37 = bf16[16,8,4096]{2,1,0:T(8,128)(2,1)} all-to-all(bf16[16,8,4096]{2,1,0:T(8,128)(2,1)S(1)} %fusion.8), channel_id=1, replica_groups=mesh['ep'=16,'tp'=2] {'ep'}, dimensions={0} | all-to-all | bytes 2097152 | tf_op jit(solution)/shard_map/all_to_all | solution.py:51
  77.4 0.0 all-gather.5.cloned.1.call-update
  77.5 0.0 reduce-scatter.2.cloned.1.call-start
  77.5 0.0 all-gather.3.cloned.1.call-done
  77.5 0.0 copy-done
  77.5 3.6 %fusion.10 = f32[256,384]{1,0:T(8,128)} fusion(bf16[256,4096]{1,0:T(8,128)(2,1)} %all-gather.3.cloned.1.call-done, bf16[1,384,4096]{2,1,0:T(8,128)(2,1)S(1)} %copy-done), kind=kOutput, calls=%fused_computation.16 | convolution fusion | flops 805306368 | bytes 5636096 | tf_op jit(solution)/shard_map/dot_general | solution.py:16
  81.1 5.8 %all-gather.5.cloned.1.call-done = bf16[256,4096]{1,0:T(8,128)(2,1)} async-done(((bf16[128,4096]{1,0:T(8,128)(2,1)}), bf16[256,4096]{1,0:T(8,128)(2,1)}) %all-gather.5.cloned.1.call-update) | async-done | bytes 2097168 | tf_op jit(solution)/shard_map/all_gather | solution.py:55
  87.0 0.0 copy-start.1
  87.0 0.0 copy-start.9
  87.0 0.0 copy-start.10
  87.0 3.9 %fusion.21 = f32[256,384]{1,0:T(8,128)S(1)} fusion(bf16[256,4096]{1,0:T(8,128)(2,1)} %all-gather.5.cloned.1.call-done, bf16[1,384,4096]{2,1,0:T(8,128)(2,1)} %param.12), kind=kOutput, calls=%fused_computation.38 | convolution fusion | flops 805306368 | bytes 5636096 | tf_op jit(solution)/shard_map/dot_general | solution.py:13
  90.9 0.0 copy-done.1
  90.9 0.1 copy-done.9
  91.1 0.0 copy-done.10
  91.1 0.0 copy-start.8
  91.1 2.0 %multiply_convert_fusion.2 = (bf16[256,384]{1,0:T(8,128)(2,1)S(1)}, bf16[256,384]{1,0:T(8,128)(2,1)S(1)}, f32[256,384]{1,0:T(8,128)}) fusion(f32[256,384]{1,0:T(8,128)S(1)} %copy-done.10, f32[256,384]{1,0:T(8,128)S(1)} %fusion.21, bf16[256,4096]{1,0:T(8,128)(2,1)S(1)} %copy-done.1, bf16[1,384,4096]{2,1,0:T(8,128)(2,1)S(1)} %copy-done.9), kind=kOutput, calls=%fused_computation.28 | convolution fusion | flops 806584320 | bytes 6815744 | tf_op jit(solution)/shard_map/dot_general | solution.py:12
  93.1 0.0 copy-start.5
  93.1 0.0 copy-start.7
  93.1 0.7 copy-done.5
  93.8 0.1 copy-done.7
  93.9 0.0 copy-done.8
  93.9 3.3 %fusion = f32[256,4096]{1,0:T(8,128)} fusion(bf16[384,4096]{1,0:T(8,128)(2,1)S(1)} %bitcast.43, bf16[384,4096]{1,0:T(8,128)(2,1)S(1)} %bitcast.44, bf16[256,384]{1,0:T(8,128)(2,1)S(1)} %get-tuple-element.5, bf16[256,384]{1,0:T(8,128)(2,1)S(1)} %get-tuple-element.4), kind=kOutput, calls=%fused_computation | convolution fusion | flops 1623982080 | bytes 10878976 | tf_op jit(solution)/shard_map/dot_general | solution.py:63
  97.2 0.0 reduce-scatter.2.cloned.1.call-update
  97.2 13.5 %reduce-scatter.2.cloned.1.call-done = f32[128,4096]{1,0:T(8,128)} async-done(((f32[256,4096]{1,0:T(8,128)}), f32[128,4096]{1,0:T(8,128)}) %reduce-scatter.2.cloned.1.call-update) | async-done | bytes 2097168 | tf_op jit(solution)/shard_map/reduce_scatter | solution.py:62
  110.7 2.7 %convert_bitcast_fusion = bf16[16,8,4096]{2,1,0:T(8,128)(2,1)} fusion(f32[128,4096]{1,0:T(8,128)} %reduce-scatter.2.cloned.1.call-done), kind=kLoop, calls=%fused_computation.19 | loop fusion | flops 524288 | bytes 3145728 | tf_op jit(solution)/shard_map/all_to_all | solution.py:68
  113.4 7.0 %all-to-all-start.2 = ((bf16[16,8,4096]{2,1,0:T(8,128)(2,1)}), bf16[16,8,4096]{2,1,0:T(8,128)(2,1)}, u32[]{:S(2)}, u32[]{:S(2)}) async-start(bf16[16,8,4096]{2,1,0:T(8,128)(2,1)} %convert_bitcast_fusion), calls=%async_computation.3 | async-start | bytes 2097152 | tf_op jit(solution)/shard_map/all_to_all | solution.py:68
  120.4 0.0 copy-start.2
  120.4 0.0 copy-start.6
  120.4 4.5 %fusion.4 = bf16[1,384,4096]{2,1,0:T(8,128)(2,1)} fusion(bf16[256,384]{1,0:T(8,128)(2,1)} %copy-done.7, bf16[256,4096]{1,0:T(8,128)(2,1)} %all-gather.5.cloned.1.call-done), kind=kOutput, calls=%fused_computation.7 | convolution fusion | flops 806879232 | bytes 5439488 | tf_op jit(solution)/shard_map/dot_general | solution.py:21
  124.9 0.0 copy-done.2
  124.9 0.0 copy-done.6
  124.9 0.0 copy-start.3
  124.9 0.0 copy-start.4
  124.9 2.7 %fusion.5 = bf16[1,384,4096]{2,1,0:T(8,128)(2,1)} fusion(bf16[256,384]{1,0:T(8,128)(2,1)S(1)} %copy-done.6, bf16[256,4096]{1,0:T(8,128)(2,1)S(1)} %copy-done.2), kind=kOutput, calls=%fused_computation.8 | convolution fusion | flops 806879232 | bytes 5439488 | tf_op jit(solution)/shard_map/dot_general | solution.py:22
  127.6 0.0 copy-done.3
  127.6 0.0 copy-done.4
  127.6 2.7 %fusion.6 = bf16[1,384,4096]{2,1,0:T(8,128)(2,1)} fusion(bf16[256,4096]{1,0:T(8,128)(2,1)S(1)} %copy-done.3, f32[256,384]{1,0:T(8,128)S(1)} %fusion.21, f32[256,384]{1,0:T(8,128)S(1)} %copy-done.4), kind=kOutput, calls=%fused_computation.9 | convolution fusion | flops 807469056 | bytes 6029312 | tf_op jit(solution)/shard_map/dot_general | solution.py:23
  130.3 15.9 %all-to-all-done.2 = bf16[16,8,4096]{2,1,0:T(8,128)(2,1)} async-done(((bf16[16,8,4096]{2,1,0:T(8,128)(2,1)}), bf16[16,8,4096]{2,1,0:T(8,128)(2,1)}, u32[]{:S(2)}, u32[]{:S(2)}) %all-to-all-start.2) | async-done | bytes 1048608 | tf_op jit(solution)/shard_map/all_to_all | solution.py:68
  146.2 2.7 %convolution_convert_fusion.3 = bf16[128,4096]{1,0:T(8,128)(2,1)} fusion(pred[128,128]{1,0:T(8,128)(4,1)S(1)} %fusion.13, bf16[16,8,4096]{2,1,0:T(8,128)(2,1)} %all-to-all-done.2), kind=kOutput, calls=%fused_computation.12 | convolution fusion | flops 134742016 | bytes 2113536 | tf_op jit(solution)/shard_map/dot_general | solution.py:72
  (1 shorter events, 0.0 us)
Async XLA Ops:
  7.2 70.4 %copy-start = (bf16[1,384,4096]{2,1,0:T(8,128)(2,1)S(1)}, bf16[1,384,4096]{2,1,0:T(8,128)(2,1)}, u32[]{:S(2)}) copy-start(bf16[1,384,4096]{2,1,0:T(8,128)(2,1)} %param.13) | copy-start | bytes 9437188
  7.2 70.3 %all-gather.3.cloned.1.call-start = ((), (), s32[]{:S(2)}) async-start(), calls=%async_computation.4 | async-start | bytes 3145728 | tf_op jit(solution)/shard_map/all_gather | solution.py:56
  46.3 40.7 %all-gather.5.cloned.1.call-start = ((), (), s32[]{:S(2)}) async-start(), calls=%async_computation.5 | async-start | bytes 3145728 | tf_op jit(solution)/shard_map/all_gather | solution.py:55
  77.5 33.2 %reduce-scatter.2.cloned.1.call-start = ((), (), s32[]{:S(2)}) async-start(), calls=%async_computation.6 | async-start | bytes 6291456 | tf_op jit(solution)/shard_map/reduce_scatter | solution.py:62
  87.0 3.9 %copy-start.1 = (bf16[256,4096]{1,0:T(8,128)(2,1)S(1)}, bf16[256,4096]{1,0:T(8,128)(2,1)}, u32[]{:S(2)}) copy-start(bf16[256,4096]{1,0:T(8,128)(2,1)} %all-gather.5.cloned.1.call-done) | copy-start | bytes 6291460
  87.0 4.1 %copy-start.9 = (bf16[1,384,4096]{2,1,0:T(8,128)(2,1)S(1)}, bf16[1,384,4096]{2,1,0:T(8,128)(2,1)}, u32[]{:S(2)}) copy-start(bf16[1,384,4096]{2,1,0:T(8,128)(2,1)} %param.11) | copy-start | bytes 9437188
  87.0 4.1 %copy-start.10 = (f32[256,384]{1,0:T(8,128)S(1)}, f32[256,384]{1,0:T(8,128)}, u32[]{:S(2)}) copy-start(f32[256,384]{1,0:T(8,128)} %fusion.10) | copy-start | bytes 1179652
  91.1 2.8 %copy-start.8 = (bf16[1,384,4096]{2,1,0:T(8,128)(2,1)S(1)}, bf16[1,384,4096]{2,1,0:T(8,128)(2,1)}, u32[]{:S(2)}) copy-start(bf16[1,384,4096]{2,1,0:T(8,128)(2,1)} %param.12) | copy-start | bytes 9437188
  93.1 0.7 copy-start.5
  93.1 0.7 copy-start.7
  113.4 32.8 %all-to-all-start.2 = ((bf16[16,8,4096]{2,1,0:T(8,128)(2,1)}), bf16[16,8,4096]{2,1,0:T(8,128)(2,1)}, u32[]{:S(2)}, u32[]{:S(2)}) async-start(bf16[16,8,4096]{2,1,0:T(8,128)(2,1)} %convert_bitcast_fusion), calls=%async_computation.3 | async-start | bytes 2097152 | tf_op jit(solution)/shard_map/all_to_all | solution.py:68
  120.4 4.5 %copy-start.2 = (bf16[256,4096]{1,0:T(8,128)(2,1)S(1)}, bf16[256,4096]{1,0:T(8,128)(2,1)}, u32[]{:S(2)}) copy-start(bf16[256,4096]{1,0:T(8,128)(2,1)} %all-gather.5.cloned.1.call-done) | copy-start | bytes 6291460
  120.4 4.5 %copy-start.6 = (bf16[256,384]{1,0:T(8,128)(2,1)S(1)}, bf16[256,384]{1,0:T(8,128)(2,1)}, u32[]{:S(2)}) copy-start(bf16[256,384]{1,0:T(8,128)(2,1)} %copy-done.5) | copy-start | bytes 589828
  124.9 2.7 %copy-start.3 = (bf16[256,4096]{1,0:T(8,128)(2,1)S(1)}, bf16[256,4096]{1,0:T(8,128)(2,1)}, u32[]{:S(2)}) copy-start(bf16[256,4096]{1,0:T(8,128)(2,1)} %all-gather.3.cloned.1.call-done) | copy-start | bytes 6291460
  124.9 2.7 %copy-start.4 = (f32[256,384]{1,0:T(8,128)S(1)}, f32[256,384]{1,0:T(8,128)}, u32[]{:S(2)}) copy-start(f32[256,384]{1,0:T(8,128)} %get-tuple-element.6) | copy-start | bytes 1179652
Sparse Core Ops, SparseCore 0:
  46.4 9.3 all-gather.2
  77.6 9.3 all-gather.4
  97.3 13.3 reduce-scatter.1
where the time goes:
time: 156 us; the launch traced here: 155 us
  blocking collectives  62.3 us (40%)
  waiting for transfers between devices  35.3 us (23%)
  matrix products  28.8 us (18%)
  between operations  13.8 us (9%)
  starting transfers between devices  7.1 us (5%)
  other arithmetic  7.04 us (5%)
    all_to_all x1, blocking collectives, local(): lax.all_to_all(send_dy, 'ep', split_axis=0, concat_axis=0, tiled=True)  32.8 us
    all_to_all x1, blocking collectives, local(): lax.all_to_all(send_x, 'ep', split_axis=0, concat_axis=0, tiled=True)  29.5 us
    all_to_all x1, waiting for transfers between devices, local(): lax.all_to_all(summed.astype(jnp.bfloat16), 'ep', split_axis=0, concat_ax...  15.9 us
    reduce_scatter x1, waiting for transfers between devices, local(): lax.psum_scatter(jnp.dot(fold_stored, joined, preferred_element_type=jnp....  13.5 us
    all_to_all x1, starting transfers between devices, local(): lax.all_to_all(summed.astype(jnp.bfloat16), 'ep', split_axis=0, concat_ax...  6.98 us
    all_gather x1, waiting for transfers between devices, local(): lax.all_gather(recv_x, 'tp', axis=0, tiled=True)  5.83 us
    dot_general x1, matrix products, expert_terms(): lax.dot_general(d_pre, rows_x, contract_first, preferred_element_type=jnp...  4.52 us
    dot_general x1, matrix products, expert_terms(): lax.dot_general(rows_x, up_rows, contract_last, preferred_element_type=jn...  3.93 us
  transfers between devices with their start and end apart: 4, of which 3 were waited for; matrix products, arithmetic and copies ran while one was open for 10% of the time, Pallas kernels for 0%

commit v1 on v0

v1 whole, which is shorter than its diff:
```python
import functools

import jax
import jax.numpy as jnp
from jax import lax
from jax.experimental import pallas as pl
from jax.experimental.pallas import tpu as pltpu
from jax.sharding import PartitionSpec as P

CAP = 8
HALF = CAP // 2
VMEM_LIMIT = 60 * 1024 * 1024

f32 = jnp.float32
bf16 = jnp.bfloat16


def low_rows(shape):
    return (lax.broadcasted_iota(jnp.int32, shape, 0) & HALF) == 0


def gather_kernel(chunk, experts, ids_ref, gates_ref, tok_ref, dy_ref, send_ref, match_ref, gate_s):
    rows, count = match_ref.shape
    topk = ids_ref.shape[0]

    @pl.when(pl.program_id(0) == 0)
    def _():
        expert_at = lax.broadcasted_iota(jnp.int32, (experts, count), 0)
        member = jnp.zeros((experts, count), f32)
        for k in range(topk):
            member += jnp.where(ids_ref[k : k + 1, :] == expert_at, 1.0, 0.0)
        earlier = jnp.where(
            lax.broadcasted_iota(jnp.int32, (count, count), 0)
            < lax.broadcasted_iota(jnp.int32, (count, count), 1),
            1.0,
            0.0,
        ).astype(bf16)
        before = jnp.dot(member.astype(bf16), earlier, preferred_element_type=f32)
        row = lax.broadcasted_iota(jnp.int32, (rows, count), 0)
        wanted = row - (row & HALF) + HALF * chunk
        match = jnp.zeros((rows, count), f32)
        gate = jnp.zeros((rows, count), f32)
        for k in range(topk):
            named = ids_ref[k : k + 1, :]
            place = jnp.sum(
                jnp.where(named == expert_at, before, 0.0), axis=0, keepdims=True
            ).astype(jnp.int32)
            target = jnp.where(named < experts, named * CAP + place, -1)
            hit = target == wanted
            match = jnp.where(hit, 1.0, match)
            gate = jnp.where(hit, gates_ref[k : k + 1, :], gate)
        match_ref[...] = match.astype(bf16)
        gate_s[...] = jnp.broadcast_to(jnp.sum(gate, axis=1, keepdims=True), gate_s.shape)

    match = match_ref[...]
    picked_x = jnp.dot(match, tok_ref[...], preferred_element_type=f32)
    picked_dy = jnp.dot(match, dy_ref[...], preferred_element_type=f32)
    out = jnp.where(low_rows(picked_x.shape), picked_x, gate_s[:, :1] * picked_dy)
    send_ref[...] = out.astype(bf16)


def gather(chunk, experts, ids, gates, tokens, grad_out):
    count, width = tokens.shape
    rows = experts * CAP
    block = width // 4
    whole = lambda i: (0, 0)
    return pl.pallas_call(
        functools.partial(gather_kernel, chunk, experts),
        grid=(width // block,),
        in_specs=[
            pl.BlockSpec(ids.shape, whole),
            pl.BlockSpec(gates.shape, whole),
            pl.BlockSpec((count, block), lambda i: (0, i)),
            pl.BlockSpec((count, block), lambda i: (0, i)),
        ],
        out_specs=[
            pl.BlockSpec((rows, block), lambda i: (0, i)),
            pl.BlockSpec((rows, count), whole),
        ],
        out_shape=[
            jax.ShapeDtypeStruct((rows, width), bf16),
            jax.ShapeDtypeStruct((rows, count), bf16),
        ],
        scratch_shapes=[pltpu.VMEM((rows, 128), f32)],
        name=f"gather_{chunk}",
        cost_estimate=pl.CostEstimate(
            flops=4 * rows * count * width, bytes_accessed=4 * width * (rows + count) * 2, transcendentals=0
        ),
        compiler_params=pltpu.CompilerParams(vmem_limit_bytes=VMEM_LIMIT),
    )(ids, gates, tokens, grad_out)


def expert_kernel(
    mine_ref, other_ref, gate_ref, up_ref, down_ref,
    own_ref, partner_ref, coef_ref,
    rows_s, joined_s, down_s, acc_s, fold_s, sems,
):
    blocks, both, block = rows_s.shape
    rows = both // 2
    hidden = down_s.shape[1]

    def copies(i):
        cols = pl.ds(pl.multiple_of(i * block, block), block)
        pairs = (
            (mine_ref.at[:, cols], rows_s.at[i, pl.ds(0, rows)]),
            (other_ref.at[:, cols], rows_s.at[i, pl.ds(rows, rows)]),
            (gate_ref.at[:, cols], joined_s.at[i, pl.ds(0, hidden)]),
            (up_ref.at[:, cols], joined_s.at[i, pl.ds(hidden, hidden)]),
            (down_ref.at[:, cols], down_s.at[i]),
        )
        return [pltpu.make_async_copy(a, b, sems.at[i, c]) for c, (a, b) in enumerate(pairs)]

    for i in range(blocks):
        for copy in copies(i):
            copy.start()

    contract_last = (((1,), (1,)), ((), ()))
    for i in range(blocks):
        for copy in copies(i):
            copy.wait()
        here = rows_s[i]
        first = lax.dot_general(here, joined_s[i], contract_last, preferred_element_type=f32)
        second = lax.dot_general(here, down_s[i], contract_last, preferred_element_type=f32)
        if i == 0:
            acc_s[:, : 2 * hidden] = first
            acc_s[:, 2 * hidden :] = second
        else:
            acc_s[:, : 2 * hidden] += first
            acc_s[:, 2 * hidden :] += second

    step = 64

    @pl.loop(0, both // step)
    def _(b):
        at = pl.ds(pl.multiple_of(b * step, step), step)
        low = low_rows((step, hidden))
        g = acc_s[at, :hidden]
        u = acc_s[at, hidden : 2 * hidden]
        a = acc_s[at, 2 * hidden :]
        g = jnp.where(low, g, pltpu.roll(g, HALF, axis=0))
        u = jnp.where(low, u, pltpu.roll(u, HALF, axis=0))
        a = jnp.where(low, pltpu.roll(a, step - HALF, axis=0), a)
        s = jax.nn.sigmoid(g)
        act = g * s * u
        d_up = a * g * s
        d_pre = a * u * s * (1.0 + g * (1.0 - s))
        zero = jnp.zeros_like(act)
        fold_s[at, :hidden] = d_pre.astype(bf16)
        fold_s[at, hidden:] = d_up.astype(bf16)
        coef_ref[at, :hidden] = jnp.where(low, d_pre, zero).astype(bf16)
        coef_ref[at, hidden : 2 * hidden] = jnp.where(low, d_up, zero).astype(bf16)
        coef_ref[at, 2 * hidden :] = jnp.where(low, zero, act).astype(bf16)

    low = low_rows((both, block))
    for i in range(blocks // 2):
        fold = fold_s[...]
        left = jnp.dot(fold, joined_s[i], preferred_element_type=f32)
        right = jnp.dot(fold, joined_s[i + blocks // 2], preferred_element_type=f32)
        out = jnp.where(low, left, right)
        own_ref[:, i * block : (i + 1) * block] = out[:rows]
        partner_ref[:, i * block : (i + 1) * block] = out[rows:].astype(bf16)


def expert_terms(mine, other, w_gate, w_up, w_down):
    rows, width = mine.shape
    hidden = w_gate.shape[0]
    blocks = 4
    block = width // blocks
    hbm = pl.BlockSpec(memory_space=pl.ANY)
    vmem = pl.BlockSpec(memory_space=pltpu.VMEM)
    return pl.pallas_call(
        expert_kernel,
        in_specs=[hbm] * 5,
        out_specs=[vmem] * 3,
        out_shape=[
            jax.ShapeDtypeStruct((rows, width // 2), f32),
            jax.ShapeDtypeStruct((rows, width // 2), bf16),
            jax.ShapeDtypeStruct((2 * rows, 3 * hidden), bf16),
        ],
        scratch_shapes=[
            pltpu.VMEM((blocks, 2 * rows, block), bf16),
            pltpu.VMEM((blocks, 2 * hidden, block), bf16),
            pltpu.VMEM((blocks, hidden, block), bf16),
            pltpu.VMEM((2 * rows, 3 * hidden), f32),
            pltpu.VMEM((2 * rows, 2 * hidden), bf16),
            pltpu.SemaphoreType.DMA((blocks, 5)),
        ],
        name="expert_terms",
        cost_estimate=pl.CostEstimate(
            flops=20 * rows * hidden * width,
            bytes_accessed=6 * hidden * width + 7 * rows * width,
            transcendentals=2 * rows * hidden,
        ),
        compiler_params=pltpu.CompilerParams(vmem_limit_bytes=VMEM_LIMIT),
    )(mine, other, w_gate, w_up, w_down)


def weight_kernel(coef_a, coef_b, mine_a, other_a, mine_b, other_b, gate_ref, up_ref, down_ref, turned):
    both = coef_a.shape[0]
    hidden = gate_ref.shape[0]

    @pl.when(pl.program_id(0) == 0)
    def _():
        turned[:, :both] = coef_a[...].T
        turned[:, both:] = coef_b[...].T

    rows = jnp.concatenate([mine_a[...], other_a[...], mine_b[...], other_b[...]], axis=0)
    for k, out in enumerate((gate_ref, up_ref, down_ref)):
        out[...] = jnp.dot(
            turned[k * hidden : (k + 1) * hidden, :], rows, preferred_element_type=f32
        ).astype(bf16)


def weight_grads(coef_a, coef_b, mine_a, other_a, mine_b, other_b):
    rows, width = mine_a.shape
    hidden = coef_a.shape[1] // 3
    block = 512
    whole = lambda i: (0, 0)
    cols = lambda i: (0, i)
    return pl.pallas_call(
        weight_kernel,
        grid=(width // block,),
        in_specs=[pl.BlockSpec(coef_a.shape, whole)] * 2 + [pl.BlockSpec((rows, block), cols)] * 4,
        out_specs=[pl.BlockSpec((hidden, block), cols)] * 3,
        out_shape=[jax.ShapeDtypeStruct((hidden, width), bf16)] * 3,
        scratch_shapes=[pltpu.VMEM((3 * hidden, 4 * rows), bf16)],
        name="weight_grads",
        cost_estimate=pl.CostEstimate(
            flops=24 * rows * hidden * width,
            bytes_accessed=6 * hidden * width + 8 * rows * width,
            transcendentals=0,
        ),
        compiler_params=pltpu.CompilerParams(vmem_limit_bytes=VMEM_LIMIT),
    )(coef_a, coef_b, mine_a, other_a, mine_b, other_b)


def combine_kernel(match_a, match_b, ret_a, ret_b, out_ref):
    low = low_rows(match_a.shape)
    keep = low == (pl.program_id(0) == 0)
    contract_first = (((0,), (0,)), ((), ()))
    total = None
    for match, ret in ((match_a, ret_a), (match_b, ret_b)):
        chosen = jnp.where(keep, match[...], jnp.zeros_like(match))
        part = lax.dot_general(chosen, ret[...], contract_first, preferred_element_type=f32)
        total = part if total is None else total + part
    out_ref[...] = total.astype(bf16)


def combine(match_a, match_b, ret_a, ret_b):
    rows, count = match_a.shape
    half = ret_a.shape[1]
    block = half // 2
    whole = lambda h, i: (0, 0)
    return pl.pallas_call(
        combine_kernel,
        grid=(2, half // block),
        in_specs=[pl.BlockSpec((rows, count), whole)] * 2
        + [pl.BlockSpec((rows, block), lambda h, i: (0, i))] * 2,
        out_specs=pl.BlockSpec((count, block), lambda h, i: (0, h * (half // block) + i)),
        out_shape=jax.ShapeDtypeStruct((count, 2 * half), bf16),
        name="combine",
        cost_estimate=pl.CostEstimate(
            flops=8 * rows * count * half, bytes_accessed=8 * rows * half, transcendentals=0
        ),
        compiler_params=pltpu.CompilerParams(vmem_limit_bytes=VMEM_LIMIT),
    )(match_a, match_b, ret_a, ret_b)


def exchange(rows, experts):
    blocks = rows.reshape(experts, CAP, rows.shape[1])
    return lax.all_to_all(blocks, "ep", split_axis=0, concat_axis=0, tiled=True).reshape(rows.shape)


def swap(value):
    return lax.ppermute(value, "tp", [(0, 1), (1, 0)])


def local(tokens, expert_ids, gate_weights, grad_out, w_gate, w_up, w_down):
    experts = lax.axis_size("ep")
    ids, gates = expert_ids.T, gate_weights.T
    weights = (w_gate[0], w_up[0], w_down[0])
    match, mine, other, coef, ret = [], [], [], [], []
    for chunk in range(2):
        send, found = gather(chunk, experts, ids, gates, tokens, grad_out)
        match.append(found)
        mine.append(exchange(send, experts))
    for chunk in range(2):
        other.append(swap(mine[chunk]))
        own, partner, terms = expert_terms(mine[chunk], other[chunk], *weights)
        coef.append(terms)
        summed = (own + swap(partner).astype(f32)).astype(bf16)
        ret.append(exchange(summed, experts))
    grads = weight_grads(coef[0], coef[1], mine[0], other[0], mine[1], other[1])
    grad_tokens = combine(match[0], match[1], ret[0], ret[1])
    return (grad_tokens, *(g[None] for g in grads))


def solution(mesh):
    rows = P(("ep", "tp"), None)
    weight = P("ep", "tp", None)
    return jax.shard_map(
        local,
        mesh=mesh,
        in_specs=(rows, rows, rows, rows, weight, weight, weight),
        out_specs=(rows, weight, weight, weight),
        check_vma=False,
    )
```

time: 156 us -> 135 us (0.87); the launches traced: 155 us -> 132 us
  blocking collectives: 62.3 us -> 0 us
  Pallas kernels: 0 us -> 42.9 us
  matrix products: 28.8 us -> 0 us
  waiting for transfers between devices: 35.3 us -> 62.8 us
  starting transfers between devices: 7.1 us -> 22.1 us
  between operations: 13.8 us -> 0.72 us
  other arithmetic: 7.04 us -> 1.81 us
    all_to_all x2 -> x0, blocking collectives: 62.3 us -> none  [the longest x1 32.8 us: local(): lax.all_to_all(send_dy, 'ep', split_axis=0, concat_axis=0, tiled=True)]
    all_to_all x1 -> x4, waiting for transfers between devices: 15.9 us -> 62.8 us  [exchange(): lax.all_to_all(blocks, 'ep', split_axis=0, concat_axis=0, tiled=True)]
    pallas_call x0 -> x6, Pallas kernels: none -> 42.9 us  [the longest x2 19.6 us: expert_terms(): pl.pallas_call(expert_kernel, in_specs=[hbm] * 5, out_specs=[vmem] * 3, o...]
    dot_general x10 -> x0, matrix products: 28.8 us -> none  [the longest x1 4.52 us: expert_terms(): lax.dot_general(d_pre, rows_x, contract_first, preferred_element_type=jnp...]
    all_to_all x1 -> x4, starting transfers between devices: 6.98 us -> 21.4 us  [exchange(): lax.all_to_all(blocks, 'ep', split_axis=0, concat_axis=0, tiled=True)]
    reduce_scatter x1 -> x0, waiting for transfers between devices: 13.5 us -> none  [local(): lax.psum_scatter(jnp.dot(fold_stored, joined, preferred_element_type=jnp....]
    all_gather x2 -> x0, waiting for transfers between devices: 5.85 us -> none  [the longest x1 5.83 us: local(): lax.all_gather(recv_x, 'tp', axis=0, tiled=True)]
    reduce_sum x3 -> x0, other arithmetic: 3.3 us -> none  [the longest x1 1.71 us: local(): jnp.sum(jnp.where(match, gate_weights[None, :, :], 0.0), axis=(1, 2))]
  transfers between devices with their start and end apart: 4 -> 8, of which waited for: 3 -> 4; matrix products, arithmetic and copies ran while one was open for 10% -> 1% of each run, Pallas kernels for 0% -> 26%
where the time goes in v1:
time: 135 us; the launch traced here: 132 us
  waiting for transfers between devices  62.8 us (47%)
  Pallas kernels  42.9 us (32%)
  starting transfers between devices  22.1 us (16%)
  local copies, waits for them, and re-layouts  1.83 us (1%)
  other arithmetic  1.81 us (1%)
    all_to_all x4, waiting for transfers between devices, exchange(): lax.all_to_all(blocks, 'ep', split_axis=0, concat_axis=0, tiled=True)  62.8 us
    all_to_all x4, starting transfers between devices, exchange(): lax.all_to_all(blocks, 'ep', split_axis=0, concat_axis=0, tiled=True)  21.4 us
    pallas_call x2, Pallas kernels, expert_terms(): pl.pallas_call(expert_kernel, in_specs=[hbm] * 5, out_specs=[vmem] * 3, o...  19.6 us
    pallas_call x1, Pallas kernels, weight_grads(): pl.pallas_call(weight_kernel, grid=(width // block,), in_specs=[pl.BlockS...  10.4 us
    pallas_call x2, Pallas kernels, gather(): pl.pallas_call(functools.partial(gather_kernel, chunk, experts), grid=(wi...  8.77 us
    pallas_call x1, Pallas kernels, combine(): pl.pallas_call(combine_kernel, grid=(2, half // block), in_specs=[pl.Bloc...  4.18 us
  transfers between devices with their start and end apart: 8, of which 4 were waited for; matrix products, arithmetic and copies ran while one was open for 1% of the time, Pallas kernels for 26%

profile of v1, /device:TPU:8, one launch (start us, length us, event | category | flops | bytes accessed | tf_op | source)
XLA Modules:
  0.0 132.2 jit_solution(12232251492177096664)
XLA Ops:
  0.6 4.4 %gather_0.1 = (bf16[128,4096]{1,0:T(8,128)(2,1)}, bf16[128,128]{1,0:T(8,128)(2,1)}) custom-call(s32[8,128]{1,0:T(8,128)} %bitcast.28, f32[8,128]{1,0:T(8,128)} %bitcast.30, bf16[128,4096]{1,0:T(8,128)(2,1)} %tok_ref.3, bf16[128,4096]{1,0:T(8,128)(2,1)} %dy_ref.3), custom_call_target="tpu_custom_call" | custom-call | flops 268435456 | bytes 8388608 | tf_op jit(solution)/shard_map/gather_0/pallas_call | solution.py:67
  5.0 7.2 %all-to-all-start = ((bf16[16,8,4096]{2,1,0:T(8,128)(2,1)}), bf16[16,8,4096]{2,1,0:T(8,128)(2,1)S(1)}, u32[]{:S(2)}, u32[]{:S(2)}) async-start(bf16[16,8,4096]{2,1,0:T(8,128)(2,1)} %bitcast.27), calls=%async_computation | async-start | bytes 2097152 | tf_op jit(solution)/shard_map/all_to_all | solution.py:271
  12.2 4.4 %gather_1.1 = (bf16[128,4096]{1,0:T(8,128)(2,1)}, bf16[128,128]{1,0:T(8,128)(2,1)}) custom-call(s32[8,128]{1,0:T(8,128)} %bitcast.29, f32[8,128]{1,0:T(8,128)} %bitcast.31, bf16[128,4096]{1,0:T(8,128)(2,1)} %tok_ref.3, bf16[128,4096]{1,0:T(8,128)(2,1)} %dy_ref.3), custom_call_target="tpu_custom_call" | custom-call | flops 268435456 | bytes 8388608 | tf_op jit(solution)/shard_map/gather_1/pallas_call | solution.py:67
  16.6 21.1 %all-to-all-done = bf16[16,8,4096]{2,1,0:T(8,128)(2,1)S(1)} async-done(((bf16[16,8,4096]{2,1,0:T(8,128)(2,1)}), bf16[16,8,4096]{2,1,0:T(8,128)(2,1)S(1)}, u32[]{:S(2)}, u32[]{:S(2)}) %all-to-all-start) | async-done | bytes 1048608 | tf_op jit(solution)/shard_map/all_to_all | solution.py:271
  37.8 0.0 copy-start.2
  37.8 4.7 %all-to-all-start.2 = ((bf16[16,8,4096]{2,1,0:T(8,128)(2,1)}), bf16[16,8,4096]{2,1,0:T(8,128)(2,1)S(1)}, u32[]{:S(2)}, u32[]{:S(2)}) async-start(bf16[16,8,4096]{2,1,0:T(8,128)(2,1)} %bitcast.26), calls=%async_computation.2 | async-start | bytes 2097152 | tf_op jit(solution)/shard_map/all_to_all | solution.py:271
  42.5 0.0 collective-permute-start
  42.5 24.1 %all-to-all-done.2 = bf16[16,8,4096]{2,1,0:T(8,128)(2,1)S(1)} async-done(((bf16[16,8,4096]{2,1,0:T(8,128)(2,1)}), bf16[16,8,4096]{2,1,0:T(8,128)(2,1)S(1)}, u32[]{:S(2)}, u32[]{:S(2)}) %all-to-all-start.2) | async-done | bytes 1048608 | tf_op jit(solution)/shard_map/all_to_all | solution.py:271
  66.6 0.0 copy-start.3
  66.6 0.0 collective-permute-start.2
  66.6 0.0 collective-permute-done.other_ref.other_a
  66.6 0.0 copy-start.6
  66.6 0.0 copy-done.2
  66.7 1.0 copy-done.6
  67.7 9.8 %expert_terms.2 = (f32[128,2048]{1,0:T(8,128)}, bf16[128,2048]{1,0:T(8,128)(2,1)}, bf16[256,1152]{1,0:T(8,128)(2,1)}) custom-call(bf16[128,4096]{1,0:T(8,128)(2,1)} %bitcast.21, bf16[128,4096]{1,0:T(8,128)(2,1)} %copy-done.6, bf16[384,4096]{1,0:T(8,128)(2,1)} %bitcast.32, bf16[384,4096]{1,0:T(8,128)(2,1)} %bitcast.34, bf16[384,4096]{1,0:T(8,128)(2,1)} %bitcast.36), custom_call_target="tpu_custom_call" | custom-call | flops 4026531840 | bytes 13107200 | tf_op jit(solution)/shard_map/expert_terms/pallas_call | solution.py:171
  77.5 0.0 copy-done.3
  77.5 0.0 copy-start.5
  77.5 0.5 collective-permute-start.1
  78.0 0.0 collective-permute-done.2.other_ref.other_b
  78.0 9.8 %expert_terms.3 = (f32[128,2048]{1,0:T(8,128)}, bf16[128,2048]{1,0:T(8,128)(2,1)}, bf16[256,1152]{1,0:T(8,128)(2,1)}) custom-call(bf16[128,4096]{1,0:T(8,128)(2,1)} %bitcast.24, bf16[128,4096]{1,0:T(8,128)(2,1)} %collective-permute-done.2.other_ref.other_b, bf16[384,4096]{1,0:T(8,128)(2,1)} %bitcast.33, bf16[384,4096]{1,0:T(8,128)(2,1)} %bitcast.35, ...), custom_call_target="tpu_custom_call" | custom-call | flops 4026531840 | bytes 13107200 | tf_op jit(solution)/shard_map/expert_terms/pallas_call | solution.py:171
  87.8 0.0 copy-start.4
  87.9 0.2 collective-permute-start.3
  88.0 0.0 collective-permute-done.1
  88.0 0.0 copy-done.5
  88.0 0.9 fusion
  88.9 4.9 %all-to-all-start.1 = ((bf16[16,8,2048]{2,1,0:T(8,128)(2,1)}), bf16[16,8,2048]{2,1,0:T(8,128)(2,1)S(1)}, u32[]{:S(2)}, u32[]{:S(2)}) async-start(bf16[16,8,2048]{2,1,0:T(8,128)(2,1)} %fusion), calls=%async_computation.1 | async-start | bytes 1048576 | tf_op jit(solution)/shard_map/all_to_all | solution.py:271
  93.8 0.0 collective-permute-done.3
  93.8 0.0 copy-done.4
  93.8 0.9 fusion.1
  94.7 14.1 %all-to-all-done.1 = bf16[16,8,2048]{2,1,0:T(8,128)(2,1)S(1)} async-done(((bf16[16,8,2048]{2,1,0:T(8,128)(2,1)}), bf16[16,8,2048]{2,1,0:T(8,128)(2,1)S(1)}, u32[]{:S(2)}, u32[]{:S(2)}) %all-to-all-start.1) | async-done | bytes 524320 | tf_op jit(solution)/shard_map/all_to_all | solution.py:271
  108.9 0.0 copy-start
  108.9 4.6 %all-to-all-start.3 = ((bf16[16,8,2048]{2,1,0:T(8,128)(2,1)}), bf16[16,8,2048]{2,1,0:T(8,128)(2,1)S(1)}, u32[]{:S(2)}, u32[]{:S(2)}) async-start(bf16[16,8,2048]{2,1,0:T(8,128)(2,1)} %fusion.1), calls=%async_computation.3 | async-start | bytes 1048576 | tf_op jit(solution)/shard_map/all_to_all | solution.py:271
  113.4 10.4 %weight_grads.1 = (bf16[384,4096]{1,0:T(8,128)(2,1)}, bf16[384,4096]{1,0:T(8,128)(2,1)}, bf16[384,4096]{1,0:T(8,128)(2,1)}) custom-call(bf16[256,1152]{1,0:T(8,128)(2,1)} %get-tuple-element.25.coef_a, bf16[256,1152]{1,0:T(8,128)(2,1)} %get-tuple-element.26.coef_b, bf16[128,4096]{1,0:T(8,128)(2,1)} %bitcast.22, bf16[128,4096]{1,0:T(8,128)(2,1)} %copy-done.6, ...), custom_call_target="tpu_custom_call" | custom-call | flops 4831838208 | bytes 13631488 | tf_op jit(solution)/shard_map/weight_grads/pallas_call | solution.py:220
  123.8 0.0 copy-done
  123.8 3.4 %all-to-all-done.3 = bf16[16,8,2048]{2,1,0:T(8,128)(2,1)S(1)} async-done(((bf16[16,8,2048]{2,1,0:T(8,128)(2,1)}), bf16[16,8,2048]{2,1,0:T(8,128)(2,1)S(1)}, u32[]{:S(2)}, u32[]{:S(2)}) %all-to-all-start.3) | async-done | bytes 524320 | tf_op jit(solution)/shard_map/all_to_all | solution.py:271
  127.2 0.0 copy-start.1
  127.2 0.8 copy-done.1
  128.0 4.2 %combine.1 = bf16[128,4096]{1,0:T(8,128)(2,1)} custom-call(bf16[128,128]{1,0:T(8,128)(2,1)} %get-tuple-element.17.match_a, bf16[128,128]{1,0:T(8,128)(2,1)} %get-tuple-element.18.match_b, bf16[128,2048]{1,0:T(8,128)(2,1)} %bitcast.18, bf16[128,2048]{1,0:T(8,128)(2,1)} %bitcast.19), custom_call_target="tpu_custom_call" | custom-call | flops 268435456 | bytes 2097152 | tf_op jit(solution)/shard_map/combine/pallas_call | solution.py:254
Async XLA Ops:
  5.0 32.8 %all-to-all-start = ((bf16[16,8,4096]{2,1,0:T(8,128)(2,1)}), bf16[16,8,4096]{2,1,0:T(8,128)(2,1)S(1)}, u32[]{:S(2)}, u32[]{:S(2)}) async-start(bf16[16,8,4096]{2,1,0:T(8,128)(2,1)} %bitcast.27), calls=%async_computation | async-start | bytes 2097152 | tf_op jit(solution)/shard_map/all_to_all | solution.py:271
  37.8 28.9 %copy-start.2 = (bf16[16,8,4096]{2,1,0:T(8,128)(2,1)}, bf16[16,8,4096]{2,1,0:T(8,128)(2,1)S(1)}, u32[]{:S(2)}) copy-start(bf16[16,8,4096]{2,1,0:T(8,128)(2,1)S(1)} %all-to-all-done) | copy-start | bytes 3145732
  37.8 28.9 %all-to-all-start.2 = ((bf16[16,8,4096]{2,1,0:T(8,128)(2,1)}), bf16[16,8,4096]{2,1,0:T(8,128)(2,1)S(1)}, u32[]{:S(2)}, u32[]{:S(2)}) async-start(bf16[16,8,4096]{2,1,0:T(8,128)(2,1)} %bitcast.26), calls=%async_computation.2 | async-start | bytes 2097152 | tf_op jit(solution)/shard_map/all_to_all | solution.py:271
  42.5 24.1 %collective-permute-start = (bf16[128,4096]{1,0:T(8,128)(2,1)S(1)}, bf16[128,4096]{1,0:T(8,128)(2,1)S(1)}, u32[]{:S(2)}, u32[]{:S(2)}) collective-permute-start(bf16[128,4096]{1,0:T(8,128)(2,1)S(1)} %bitcast.20), channel_id=1, source_target_pairs={{0,1},{1,0},{2,3},{3,2},{4,5},{5,4},{6,7},{7,6},{8,9},{9,8},{10,11... | collective-permute-start | bytes 3145736 | tf_op jit(solution)/shard_map/ppermute | solution.py:275
  66.6 10.8 %copy-start.3 = (bf16[16,8,4096]{2,1,0:T(8,128)(2,1)}, bf16[16,8,4096]{2,1,0:T(8,128)(2,1)S(1)}, u32[]{:S(2)}) copy-start(bf16[16,8,4096]{2,1,0:T(8,128)(2,1)S(1)} %all-to-all-done.2) | copy-start | bytes 3145732
  66.6 11.4 %collective-permute-start.2 = (bf16[128,4096]{1,0:T(8,128)(2,1)S(1)}, bf16[128,4096]{1,0:T(8,128)(2,1)}, u32[]{:S(2)}, u32[]{:S(2)}) collective-permute-start(bf16[128,4096]{1,0:T(8,128)(2,1)S(1)} %bitcast.23), channel_id=1, source_target_pairs={{0,1},{1,0},{2,3},{3,2},{4,5},{5,4},{6,7},{7,6},{8,9},{9,8},{10,11... | collective-permute-start | bytes 3145736 | tf_op jit(solution)/shard_map/ppermute | solution.py:275
  66.6 1.0 copy-start.6
  77.5 10.5 %copy-start.5 = (f32[128,2048]{1,0:T(8,128)S(1)}, f32[128,2048]{1,0:T(8,128)}, u32[]{:S(2)}) copy-start(f32[128,2048]{1,0:T(8,128)} %get-tuple-element.20) | copy-start | bytes 3145732
  77.5 10.5 %collective-permute-start.1 = (bf16[128,2048]{1,0:T(8,128)(2,1)}, bf16[128,2048]{1,0:T(8,128)(2,1)S(1)}, u32[]{:S(2)}, u32[]{:S(2)}) collective-permute-start(bf16[128,2048]{1,0:T(8,128)(2,1)} %get-tuple-element.21), channel_id=1, source_target_pairs={{0,1},{1,0},{2,3},{3,2},{4,5},{5,4},{6,7},{7,6},{8,9},{9,8},{10,11... | collective-permute-start | bytes 1572872 | tf_op jit(solution)/shard_map/ppermute | solution.py:275
  87.8 6.0 %copy-start.4 = (f32[128,2048]{1,0:T(8,128)S(1)}, f32[128,2048]{1,0:T(8,128)}, u32[]{:S(2)}) copy-start(f32[128,2048]{1,0:T(8,128)} %get-tuple-element.23) | copy-start | bytes 3145732
  87.9 6.0 %collective-permute-start.3 = (bf16[128,2048]{1,0:T(8,128)(2,1)}, bf16[128,2048]{1,0:T(8,128)(2,1)S(1)}, u32[]{:S(2)}, u32[]{:S(2)}) collective-permute-start(bf16[128,2048]{1,0:T(8,128)(2,1)} %get-tuple-element.24), channel_id=1, source_target_pairs={{0,1},{1,0},{2,3},{3,2},{4,5},{5,4},{6,7},{7,6},{8,9},{9,8},{10,11... | collective-permute-start | bytes 1572872 | tf_op jit(solution)/shard_map/ppermute | solution.py:275
  88.9 19.9 %all-to-all-start.1 = ((bf16[16,8,2048]{2,1,0:T(8,128)(2,1)}), bf16[16,8,2048]{2,1,0:T(8,128)(2,1)S(1)}, u32[]{:S(2)}, u32[]{:S(2)}) async-start(bf16[16,8,2048]{2,1,0:T(8,128)(2,1)} %fusion), calls=%async_computation.1 | async-start | bytes 1048576 | tf_op jit(solution)/shard_map/all_to_all | solution.py:271
  108.9 14.9 %copy-start = (bf16[16,8,2048]{2,1,0:T(8,128)(2,1)}, bf16[16,8,2048]{2,1,0:T(8,128)(2,1)S(1)}, u32[]{:S(2)}) copy-start(bf16[16,8,2048]{2,1,0:T(8,128)(2,1)S(1)} %all-to-all-done.1) | copy-start | bytes 1572868
  108.9 18.3 %all-to-all-start.3 = ((bf16[16,8,2048]{2,1,0:T(8,128)(2,1)}), bf16[16,8,2048]{2,1,0:T(8,128)(2,1)S(1)}, u32[]{:S(2)}, u32[]{:S(2)}) async-start(bf16[16,8,2048]{2,1,0:T(8,128)(2,1)} %fusion.1), calls=%async_computation.3 | async-start | bytes 1048576 | tf_op jit(solution)/shard_map/all_to_all | solution.py:271
  127.2 0.8 copy-start.1

commit v2 on v1

--- a/solution.py
+++ b/solution.py
@@ -7,9 +7,10 @@
 from jax.experimental.pallas import tpu as pltpu
 from jax.sharding import PartitionSpec as P
 
+
 CAP = 8
 HALF = CAP // 2
-VMEM_LIMIT = 60 * 1024 * 1024
+VMEM_LIMIT = 65472 * 1024
 
 f32 = jnp.float32
 bf16 = jnp.bfloat16
@@ -82,9 +83,8 @@
             jax.ShapeDtypeStruct((rows, count), bf16),
         ],
         scratch_shapes=[pltpu.VMEM((rows, 128), f32)],
-        name=f"gather_{chunk}",
         cost_estimate=pl.CostEstimate(
-            flops=4 * rows * count * width, bytes_accessed=4 * width * (rows + count) * 2, transcendentals=0
+            flops=4 * rows * count * width, bytes_accessed=2 * width * (rows + 2 * count), transcendentals=0
         ),
         compiler_params=pltpu.CompilerParams(vmem_limit_bytes=VMEM_LIMIT),
     )(ids, gates, tokens, grad_out)
@@ -166,11 +166,12 @@
     hidden = w_gate.shape[0]
     blocks = 4
     block = width // blocks
+    anywhere = pl.BlockSpec(memory_space=pl.ANY)
     hbm = pl.BlockSpec(memory_space=pl.ANY)
     vmem = pl.BlockSpec(memory_space=pltpu.VMEM)
     return pl.pallas_call(
         expert_kernel,
-        in_specs=[hbm] * 5,
+        in_specs=[anywhere] * 2 + [hbm] * 3,
         out_specs=[vmem] * 3,
         out_shape=[
             jax.ShapeDtypeStruct((rows, width // 2), f32),
@@ -260,15 +261,14 @@
         out_shape=jax.ShapeDtypeStruct((count, 2 * half), bf16),
         name="combine",
         cost_estimate=pl.CostEstimate(
-            flops=8 * rows * count * half, bytes_accessed=8 * rows * half, transcendentals=0
+            flops=8 * rows * count * half, bytes_accessed=4 * (rows + count) * half, transcendentals=0
         ),
         compiler_params=pltpu.CompilerParams(vmem_limit_bytes=VMEM_LIMIT),
     )(match_a, match_b, ret_a, ret_b)
 
 
-def exchange(rows, experts):
-    blocks = rows.reshape(experts, CAP, rows.shape[1])
-    return lax.all_to_all(blocks, "ep", split_axis=0, concat_axis=0, tiled=True).reshape(rows.shape)
+def exchange(rows):
+    return lax.all_to_all(rows, "ep", split_axis=0, concat_axis=0, tiled=True)
 
 
 def swap(value):
@@ -283,13 +283,14 @@
     for chunk in range(2):
         send, found = gather(chunk, experts, ids, gates, tokens, grad_out)
         match.append(found)
-        mine.append(exchange(send, experts))
+        mine.append(exchange(send))
     for chunk in range(2):
         other.append(swap(mine[chunk]))
         own, partner, terms = expert_terms(mine[chunk], other[chunk], *weights)
         coef.append(terms)
-        summed = (own + swap(partner).astype(f32)).astype(bf16)
-        ret.append(exchange(summed, experts))
+        theirs = swap(partner)
+        summed = (own + theirs.astype(f32)).astype(bf16)
+        ret.append(exchange(summed))
     grads = weight_grads(coef[0], coef[1], mine[0], other[0], mine[1], other[1])
     grad_tokens = combine(match[0], match[1], ret[0], ret[1])
     return (grad_tokens, *(g[None] for g in grads))

time: 135 us -> 135 us (level)
  local copies, waits for them, and re-layouts: 1.83 us -> 0.01 us
  other arithmetic: 1.81 us -> 3.23 us
    all_to_all x0 -> x2, other arithmetic: none -> 3.23 us  [exchange(): return lax.all_to_all(rows, 'ep', split_axis=0, concat_axis=0, tiled=True)]
    unnamed x14 -> x2, local copies, waits for them, and re-layouts: 1.83 us -> 0.01 us
    reshape x2 -> x0, other arithmetic: 1.81 us -> none  [exchange(): blocks = rows.reshape(experts, CAP, rows.shape[1])]
  transfers between devices with their start and end apart: 8 -> 8, of which waited for: 4 -> 4; matrix products, arithmetic and copies ran while one was open for 1% -> 2% of each run, Pallas kernels for 26% -> 26%
where the time goes in v2:
time: 135 us; the launch traced here: 132 us
  waiting for transfers between devices  63.2 us (47%)
  Pallas kernels  42.9 us (32%)
  starting transfers between devices  22.1 us (16%)
  other arithmetic  3.23 us (2%)
    all_to_all x4, waiting for transfers between devices, exchange(): return lax.all_to_all(rows, 'ep', split_axis=0, concat_axis=0, tiled=True)  63.2 us
    all_to_all x4, starting transfers between devices, exchange(): return lax.all_to_all(rows, 'ep', split_axis=0, concat_axis=0, tiled=True)  21.4 us
    pallas_call x2, Pallas kernels, expert_terms(): pl.pallas_call(expert_kernel, in_specs=[anywhere] * 2 + [hbm] * 3, out_sp...  19.6 us
    pallas_call x1, Pallas kernels, weight_grads(): pl.pallas_call(weight_kernel, grid=(width // block,), in_specs=[pl.BlockS...  10.4 us
    pallas_call x2, Pallas kernels, gather(): pl.pallas_call(functools.partial(gather_kernel, chunk, experts), grid=(wi...  8.77 us
    pallas_call x1, Pallas kernels, combine(): pl.pallas_call(combine_kernel, grid=(2, half // block), in_specs=[pl.Bloc...  4.18 us
    all_to_all x2, other arithmetic, exchange(): return lax.all_to_all(rows, 'ep', split_axis=0, concat_axis=0, tiled=True)  3.23 us
  transfers between devices with their start and end apart: 8, of which 4 were waited for; matrix products, arithmetic and copies ran while one was open for 2% of the time, Pallas kernels for 26%

profile of v2, /device:TPU:8, one launch (start us, length us, event | category | flops | bytes accessed | tf_op | source)
XLA Modules:
  0.0 132.2 jit_solution(14026363478414953542)
XLA Ops:
  0.6 4.4 %shard_map.102 = (bf16[128,4096]{1,0:T(8,128)(2,1)}, bf16[128,128]{1,0:T(8,128)(2,1)}) custom-call(s32[8,128]{1,0:T(8,128)} %bitcast.20, f32[8,128]{1,0:T(8,128)} %bitcast.22, bf16[128,4096]{1,0:T(8,128)(2,1)} %tok_ref.3, bf16[128,4096]{1,0:T(8,128)(2,1)} %dy_ref.3), custom_call_target="tpu_custom_call" | custom-call | flops 268435456 | bytes 3145728 | tf_op jit(solution)/shard_map/pallas_call | solution.py:68
  5.0 7.2 %all-to-all-start = ((bf16[16,8,4096]{2,1,0:T(8,128)(2,1)}), bf16[16,8,4096]{2,1,0:T(8,128)(2,1)}, u32[]{:S(2)}, u32[]{:S(2)}) async-start(bf16[16,8,4096]{2,1,0:T(8,128)(2,1)} %bitcast.19), calls=%async_computation | async-start | bytes 2097152 | tf_op jit(solution)/shard_map/all_to_all | solution.py:271
  12.2 4.4 %shard_map.103 = (bf16[128,4096]{1,0:T(8,128)(2,1)}, bf16[128,128]{1,0:T(8,128)(2,1)}) custom-call(s32[8,128]{1,0:T(8,128)} %bitcast.21, f32[8,128]{1,0:T(8,128)} %bitcast.23, bf16[128,4096]{1,0:T(8,128)(2,1)} %tok_ref.3, bf16[128,4096]{1,0:T(8,128)(2,1)} %dy_ref.3), custom_call_target="tpu_custom_call" | custom-call | flops 268435456 | bytes 3145728 | tf_op jit(solution)/shard_map/pallas_call | solution.py:68
  16.6 21.2 %all-to-all-done = bf16[16,8,4096]{2,1,0:T(8,128)(2,1)} async-done(((bf16[16,8,4096]{2,1,0:T(8,128)(2,1)}), bf16[16,8,4096]{2,1,0:T(8,128)(2,1)}, u32[]{:S(2)}, u32[]{:S(2)}) %all-to-all-start) | async-done | bytes 1048608 | tf_op jit(solution)/shard_map/all_to_all | solution.py:271
  37.9 4.7 %all-to-all-start.2 = ((bf16[16,8,4096]{2,1,0:T(8,128)(2,1)}), bf16[16,8,4096]{2,1,0:T(8,128)(2,1)}, u32[]{:S(2)}, u32[]{:S(2)}) async-start(bf16[16,8,4096]{2,1,0:T(8,128)(2,1)} %bitcast.18), calls=%async_computation.2 | async-start | bytes 2097152 | tf_op jit(solution)/shard_map/all_to_all | solution.py:271
  42.6 0.0 collective-permute-start
  42.6 24.2 %all-to-all-done.2 = bf16[16,8,4096]{2,1,0:T(8,128)(2,1)} async-done(((bf16[16,8,4096]{2,1,0:T(8,128)(2,1)}), bf16[16,8,4096]{2,1,0:T(8,128)(2,1)}, u32[]{:S(2)}, u32[]{:S(2)}) %all-to-all-start.2) | async-done | bytes 1048608 | tf_op jit(solution)/shard_map/all_to_all | solution.py:271
  66.8 0.0 collective-permute-start.2
  66.8 0.0 collective-permute-done.other_ref.other_a
  66.8 9.8 %expert_terms.2 = (f32[128,2048]{1,0:T(8,128)}, bf16[128,2048]{1,0:T(8,128)(2,1)}, bf16[256,1152]{1,0:T(8,128)(2,1)}) custom-call(bf16[128,4096]{1,0:T(8,128)(2,1)} %bitcast.3.mine_ref.mine_a, bf16[128,4096]{1,0:T(8,128)(2,1)} %collective-permute-done.other_ref.other_a, bf16[384,4096]{1,0:T(8,128)(2,1)} %bitcast.24, bf16[384,4096]{1,0:T(8,128)(2,1)} %bitcast.26, ...), custom_call_target="tpu_custom_call" | custom-call | flops 4026531840 | bytes 13107200 | tf_op jit(solution)/shard_map/expert_terms/pallas_call | solution.py:172
  76.7 0.6 collective-permute-start.1
  77.2 0.0 collective-permute-done.2.other_ref.other_b
  77.2 9.8 %expert_terms.3 = (f32[128,2048]{1,0:T(8,128)}, bf16[128,2048]{1,0:T(8,128)(2,1)}, bf16[256,1152]{1,0:T(8,128)(2,1)}) custom-call(bf16[128,4096]{1,0:T(8,128)(2,1)} %bitcast.10.mine_ref.mine_b, bf16[128,4096]{1,0:T(8,128)(2,1)} %collective-permute-done.2.other_ref.other_b, bf16[384,4096]{1,0:T(8,128)(2,1)} %bitcast.25, bf16[384,4096]{1,0:T(8,128)(2,1)} %bitcast.27, ...), custom_call_target="tpu_custom_call" | custom-call | flops 4026531840 | bytes 13107200 | tf_op jit(solution)/shard_map/expert_terms/pallas_call | solution.py:172
  87.1 0.0 copy-start
  87.1 0.1 collective-permute-start.3
  87.2 0.0 collective-permute-done.1
  87.2 2.3 %fusion = bf16[16,8,2048]{2,1,0:T(8,128)(2,1)} fusion(f32[128,2048]{1,0:T(8,128)} %get-tuple-element.20, bf16[128,2048]{1,0:T(8,128)(2,1)} %collective-permute-done.1), kind=kLoop, calls=%fused_computation.2 | loop fusion | flops 786432 | bytes 2097152 | tf_op jit(solution)/shard_map/all_to_all | solution.py:271
  89.5 4.9 %all-to-all-start.1 = ((bf16[16,8,2048]{2,1,0:T(8,128)(2,1)}), bf16[16,8,2048]{2,1,0:T(8,128)(2,1)}, u32[]{:S(2)}, u32[]{:S(2)}) async-start(bf16[16,8,2048]{2,1,0:T(8,128)(2,1)} %fusion), calls=%async_computation.1 | async-start | bytes 1048576 | tf_op jit(solution)/shard_map/all_to_all | solution.py:271
  94.4 0.0 collective-permute-done.3
  94.4 0.0 copy-done
  94.4 0.9 fusion.1
  95.3 14.2 %all-to-all-done.1 = bf16[16,8,2048]{2,1,0:T(8,128)(2,1)} async-done(((bf16[16,8,2048]{2,1,0:T(8,128)(2,1)}), bf16[16,8,2048]{2,1,0:T(8,128)(2,1)}, u32[]{:S(2)}, u32[]{:S(2)}) %all-to-all-start.1) | async-done | bytes 524320 | tf_op jit(solution)/shard_map/all_to_all | solution.py:271
  109.5 4.6 %all-to-all-start.3 = ((bf16[16,8,2048]{2,1,0:T(8,128)(2,1)}), bf16[16,8,2048]{2,1,0:T(8,128)(2,1)}, u32[]{:S(2)}, u32[]{:S(2)}) async-start(bf16[16,8,2048]{2,1,0:T(8,128)(2,1)} %fusion.1), calls=%async_computation.3 | async-start | bytes 1048576 | tf_op jit(solution)/shard_map/all_to_all | solution.py:271
  114.1 10.4 %weight_grads.1 = (bf16[384,4096]{1,0:T(8,128)(2,1)}, bf16[384,4096]{1,0:T(8,128)(2,1)}, bf16[384,4096]{1,0:T(8,128)(2,1)}) custom-call(bf16[256,1152]{1,0:T(8,128)(2,1)} %get-tuple-element.25.coef_a, bf16[256,1152]{1,0:T(8,128)(2,1)} %get-tuple-element.26.coef_b, bf16[128,4096]{1,0:T(8,128)(2,1)} %bitcast.3.mine_ref.mine_a, ...), custom_call_target="tpu_custom_call" | custom-call | flops 4831838208 | bytes 13631488 | tf_op jit(solution)/shard_map/weight_grads/pallas_call | solution.py:221
  124.5 3.5 %all-to-all-done.3 = bf16[16,8,2048]{2,1,0:T(8,128)(2,1)} async-done(((bf16[16,8,2048]{2,1,0:T(8,128)(2,1)}), bf16[16,8,2048]{2,1,0:T(8,128)(2,1)}, u32[]{:S(2)}, u32[]{:S(2)}) %all-to-all-start.3) | async-done | bytes 524320 | tf_op jit(solution)/shard_map/all_to_all | solution.py:271
  128.0 4.2 %combine.1 = bf16[128,4096]{1,0:T(8,128)(2,1)} custom-call(bf16[128,128]{1,0:T(8,128)(2,1)} %get-tuple-element.17.match_a, bf16[128,128]{1,0:T(8,128)(2,1)} %get-tuple-element.18.match_b, bf16[128,2048]{1,0:T(8,128)(2,1)} %bitcast.8.ret_a, bf16[128,2048]{1,0:T(8,128)(2,1)} %bitcast.12.ret_b), custom_call_target="tpu_custom_call" | custom-call | flops 268435456 | bytes 2097152 | tf_op jit(solution)/shard_map/combine/pallas_call | solution.py:255
Async XLA Ops:
  5.0 32.9 %all-to-all-start = ((bf16[16,8,4096]{2,1,0:T(8,128)(2,1)}), bf16[16,8,4096]{2,1,0:T(8,128)(2,1)}, u32[]{:S(2)}, u32[]{:S(2)}) async-start(bf16[16,8,4096]{2,1,0:T(8,128)(2,1)} %bitcast.19), calls=%async_computation | async-start | bytes 2097152 | tf_op jit(solution)/shard_map/all_to_all | solution.py:271
  37.9 29.0 %all-to-all-start.2 = ((bf16[16,8,4096]{2,1,0:T(8,128)(2,1)}), bf16[16,8,4096]{2,1,0:T(8,128)(2,1)}, u32[]{:S(2)}, u32[]{:S(2)}) async-start(bf16[16,8,4096]{2,1,0:T(8,128)(2,1)} %bitcast.18), calls=%async_computation.2 | async-start | bytes 2097152 | tf_op jit(solution)/shard_map/all_to_all | solution.py:271
  42.6 24.2 %collective-permute-start = (bf16[128,4096]{1,0:T(8,128)(2,1)}, bf16[128,4096]{1,0:T(8,128)(2,1)}, u32[]{:S(2)}, u32[]{:S(2)}) collective-permute-start(bf16[128,4096]{1,0:T(8,128)(2,1)} %bitcast.3.mine_ref.mine_a), channel_id=1, source_target_pairs={{0,1},{1,0},{2,3},{3,2},{4,5},{5,4},{6,7},{7,6},{8,9},{9,8},{10,11... | collective-permute-start | bytes 3145736 | tf_op jit(solution)/shard_map/ppermute | solution.py:275
  66.8 10.4 %collective-permute-start.2 = (bf16[128,4096]{1,0:T(8,128)(2,1)}, bf16[128,4096]{1,0:T(8,128)(2,1)}, u32[]{:S(2)}, u32[]{:S(2)}) collective-permute-start(bf16[128,4096]{1,0:T(8,128)(2,1)} %bitcast.10.mine_ref.mine_b), channel_id=1, source_target_pairs={{0,1},{1,0},{2,3},{3,2},{4,5},{5,4},{6,7},{7,6},{8,9},{9,8},{10,11... | collective-permute-start | bytes 3145736 | tf_op jit(solution)/shard_map/ppermute | solution.py:275
  76.7 10.5 %collective-permute-start.1 = (bf16[128,2048]{1,0:T(8,128)(2,1)}, bf16[128,2048]{1,0:T(8,128)(2,1)}, u32[]{:S(2)}, u32[]{:S(2)}) collective-permute-start(bf16[128,2048]{1,0:T(8,128)(2,1)} %get-tuple-element.21), channel_id=1, source_target_pairs={{0,1},{1,0},{2,3},{3,2},{4,5},{5,4},{6,7},{7,6},{8,9},{9,8},{10,11... | collective-permute-start | bytes 1572872 | tf_op jit(solution)/shard_map/ppermute | solution.py:275
  87.1 7.3 %copy-start = (f32[128,2048]{1,0:T(8,128)S(1)}, f32[128,2048]{1,0:T(8,128)}, u32[]{:S(2)}) copy-start(f32[128,2048]{1,0:T(8,128)} %get-tuple-element.23) | copy-start | bytes 3145732
  87.1 7.3 %collective-permute-start.3 = (bf16[128,2048]{1,0:T(8,128)(2,1)}, bf16[128,2048]{1,0:T(8,128)(2,1)S(1)}, u32[]{:S(2)}, u32[]{:S(2)}) collective-permute-start(bf16[128,2048]{1,0:T(8,128)(2,1)} %get-tuple-element.24), channel_id=1, source_target_pairs={{0,1},{1,0},{2,3},{3,2},{4,5},{5,4},{6,7},{7,6},{8,9},{9,8},{10,11... | collective-permute-start | bytes 1572872 | tf_op jit(solution)/shard_map/ppermute | solution.py:275
  89.5 20.0 %all-to-all-start.1 = ((bf16[16,8,2048]{2,1,0:T(8,128)(2,1)}), bf16[16,8,2048]{2,1,0:T(8,128)(2,1)}, u32[]{:S(2)}, u32[]{:S(2)}) async-start(bf16[16,8,2048]{2,1,0:T(8,128)(2,1)} %fusion), calls=%async_computation.1 | async-start | bytes 1048576 | tf_op jit(solution)/shard_map/all_to_all | solution.py:271
  109.5 18.4 %all-to-all-start.3 = ((bf16[16,8,2048]{2,1,0:T(8,128)(2,1)}), bf16[16,8,2048]{2,1,0:T(8,128)(2,1)}, u32[]{:S(2)}, u32[]{:S(2)}) async-start(bf16[16,8,2048]{2,1,0:T(8,128)(2,1)} %fusion.1), calls=%async_computation.3 | async-start | bytes 1048576 | tf_op jit(solution)/shard_map/all_to_all | solution.py:271

commit v3 on v0

v3 whole, which is shorter than its diff:
```python
import functools

import jax
import jax.numpy as jnp
from jax import lax
from jax.experimental import pallas as pl
from jax.experimental.pallas import tpu as pltpu
from jax.sharding import PartitionSpec as P


CAP = 8
MIB = 1 << 20

f32 = jnp.float32
bf16 = jnp.bfloat16


def in_hbm(x):
    return pltpu.with_memory_space_constraint(x, pltpu.HBM)


def in_vmem(x):
    return pltpu.with_memory_space_constraint(x, pltpu.VMEM)


def route(experts, ids_ref, gates_ref, match_ref, gate_s):
    rows, count = match_ref.shape
    expert_at = lax.broadcasted_iota(jnp.int32, (experts, count), 0)
    member = jnp.zeros((experts, count), f32)
    for k in range(ids_ref.shape[0]):
        member += jnp.where(ids_ref[k : k + 1, :] == expert_at, 1.0, 0.0)
    earlier = jnp.where(
        lax.broadcasted_iota(jnp.int32, (count, count), 0)
        < lax.broadcasted_iota(jnp.int32, (count, count), 1),
        1.0,
        0.0,
    ).astype(bf16)
    before = jnp.dot(member.astype(bf16), earlier, preferred_element_type=f32)
    row = lax.broadcasted_iota(jnp.int32, (rows, count), 0)
    match = jnp.zeros((rows, count), f32)
    gate = jnp.zeros((rows, count), f32)
    for k in range(ids_ref.shape[0]):
        named = ids_ref[k : k + 1, :]
        place = jnp.sum(
            jnp.where(named == expert_at, before, 0.0), axis=0, keepdims=True
        ).astype(jnp.int32)
        hit = jnp.where(named < experts, named * CAP + place, -1) == row
        match = jnp.where(hit, 1.0, match)
        gate = jnp.where(hit, gates_ref[k : k + 1, :], gate)
    match_ref[...] = match.astype(bf16)
    gate_s[...] = jnp.broadcast_to(jnp.sum(gate, axis=1, keepdims=True), gate_s.shape)


def gather_kernel(experts, half, ids_ref, gates_ref, tok_ref, dy_ref, send_ref, match_ref, gate_s):
    step = pl.program_id(0)

    @pl.when(step == 0)
    def _():
        route(experts, ids_ref, gates_ref, match_ref, gate_s)

    @pl.when(step < half)
    def _():
        send_ref[...] = jnp.dot(
            match_ref[...], tok_ref[...], preferred_element_type=f32
        ).astype(bf16)

    @pl.when(step >= half)
    def _():
        picked = jnp.dot(match_ref[...], dy_ref[...], preferred_element_type=f32)
        send_ref[...] = (gate_s[:, :1] * picked).astype(bf16)


def gather(experts, ids, gates, tokens, grad_out):
    count, width = tokens.shape
    rows = experts * CAP
    half = 2
    block = width // half
    whole = lambda i: (0, 0)
    return pl.pallas_call(
        functools.partial(gather_kernel, experts, half),
        grid=(2 * half,),
        in_specs=[
            pl.BlockSpec(ids.shape, whole),
            pl.BlockSpec(gates.shape, whole),
            pl.BlockSpec((count, block), lambda i: (0, jnp.minimum(i, half - 1))),
            pl.BlockSpec((count, block), lambda i: (0, jnp.maximum(i - half, 0))),
        ],
        out_specs=[
            pl.BlockSpec((rows, block), lambda i: (0, i)),
            pl.BlockSpec((rows, count), whole),
        ],
        out_shape=[
            pltpu.HBM((rows, 2 * width), bf16),
            jax.ShapeDtypeStruct((rows, count), bf16),
        ],
        scratch_shapes=[pltpu.VMEM((rows, 128), f32)],
        name="gather",
        cost_estimate=pl.CostEstimate(
            flops=4 * rows * count * width, bytes_accessed=4 * width * (rows + count), transcendentals=0
        ),
        compiler_params=pltpu.CompilerParams(vmem_limit_bytes=12 * MIB + 16 * rows * block),
    )(in_hbm(ids), in_hbm(gates), in_hbm(tokens), in_hbm(grad_out))


def expert_kernel(
    recv_ref, gate_a, up_a, down_a, gate_b, up_b, down_b, ret_ref, own_ref, partner_ref,
    joined_s, down_s, acc_s, out_s, sems, out_sems,
):
    chunks, chunk = down_s.shape[:2]
    width = acc_s.shape[1]
    hidden = gate_a.shape[0]
    half = chunks // 2

    def load(c, refs):
        at = pl.ds((c % half) * chunk, chunk)
        dsts = (joined_s.at[c, pl.ds(0, chunk)], joined_s.at[c, pl.ds(chunk, chunk)], down_s.at[c])
        return [
            pltpu.make_async_copy(ref.at[at], dst, sems.at[c, k])
            for k, (ref, dst) in enumerate(zip(refs, dsts))
        ]

    own, partner = (gate_a, up_a, down_a), (gate_b, up_b, down_b)
    for c in range(chunks):
        for copy in load(c, own if c < half else partner):
            copy.start()

    contract_last = (((1,), (1,)), ((), ()))
    blocks = out_s.shape[0]
    block = width // blocks
    for h, coef_ref in enumerate((own_ref, partner_ref)):

        @pl.loop(0, half)
        def _(b):
            c = h * half + b
            for k, dst in enumerate(
                (joined_s.at[c, pl.ds(0, chunk)], joined_s.at[c, pl.ds(chunk, chunk)], down_s.at[c])
            ):
                pltpu.make_async_copy(gate_a.at[pl.ds(0, chunk)], dst, sems.at[c, k]).wait()
            both = lax.dot_general(
                recv_ref[:, :width], joined_s[c], contract_last, preferred_element_type=f32
            )
            a = lax.dot_general(
                recv_ref[:, width:], down_s[c], contract_last, preferred_element_type=f32
            )
            g, u = both[:, :chunk], both[:, chunk:]
            s = jax.nn.sigmoid(g)
            d_pre = (a * u * s * (1.0 + g * (1.0 - s))).astype(bf16)
            d_up = (a * g * s).astype(bf16)
            at = b * chunk
            coef_ref[:, pl.ds(pl.multiple_of(at, chunk), chunk)] = d_pre
            coef_ref[:, pl.ds(pl.multiple_of(hidden + at, chunk), chunk)] = d_up
            coef_ref[:, pl.ds(pl.multiple_of(2 * hidden + at, chunk), chunk)] = (g * s * u).astype(bf16)
            fold = jnp.concatenate([d_pre, d_up], axis=1)
            for i in range(blocks):
                cols = slice(i * block, (i + 1) * block)
                part = jnp.dot(fold, joined_s[c, :, cols], preferred_element_type=f32)
                if h:
                    acc_s[:, cols] += part
                    continue

                @pl.when(b == 0)
                def _():
                    acc_s[:, cols] = part

                @pl.when(b > 0)
                def _():
                    acc_s[:, cols] += part

    def store(i):
        return pltpu.make_async_copy(
            out_s.at[i], ret_ref.at[:, pl.ds(i * block, block)], out_sems.at[i]
        )

    for i in range(blocks):
        out_s[i] = acc_s[:, i * block : (i + 1) * block].astype(bf16)
        store(i).start()
    for i in range(blocks):
        store(i).wait()


def expert_terms(recv, own, partner):
    rows, width = recv.shape[0], recv.shape[1] // 2
    hidden = own[0].shape[0]
    chunk = 128
    chunks = 2 * hidden // chunk
    blocks = 4
    anywhere = pl.BlockSpec(memory_space=pl.ANY)
    vmem = pl.BlockSpec(memory_space=pltpu.VMEM)
    coef = jax.ShapeDtypeStruct((rows, 3 * hidden), bf16)
    return pl.pallas_call(
        expert_kernel,
        in_specs=[vmem] + [anywhere] * 6,
        out_specs=[anywhere, vmem, vmem],
        out_shape=[pltpu.HBM((rows, width), bf16), coef, coef],
        scratch_shapes=[
            pltpu.VMEM((chunks, 2 * chunk, width), bf16),
            pltpu.VMEM((chunks, chunk, width), bf16),
            pltpu.VMEM((rows, width), f32),
            pltpu.VMEM((blocks, rows, width // blocks), bf16),
            pltpu.SemaphoreType.DMA((chunks, 3)),
            pltpu.SemaphoreType.DMA((blocks,)),
        ],
        name="expert_terms",
        cost_estimate=pl.CostEstimate(
            flops=20 * rows * hidden * width,
            bytes_accessed=12 * hidden * width + 6 * rows * width,
            transcendentals=2 * rows * hidden,
        ),
        compiler_params=pltpu.CompilerParams(
            vmem_limit_bytes=8 * MIB + 12 * hidden * width + 8 * rows * width
        ),
    )(in_vmem(recv), *(in_hbm(w) for w in (*own, *partner)))


def weight_kernel(coef_a, coef_b, x_a, dy_a, x_b, dy_b, gate_ref, up_ref, down_ref, turned):
    rows = coef_a.shape[0]
    hidden = gate_ref.shape[0]

    @pl.when(pl.program_id(0) == 0)
    def _():
        turned[:, :rows] = coef_a[...].T
        turned[:, rows:] = coef_b[...].T

    x = jnp.concatenate([x_a[...], x_b[...]], axis=0)
    dy = jnp.concatenate([dy_a[...], dy_b[...]], axis=0)
    for k, (out, right) in enumerate(((gate_ref, x), (up_ref, x), (down_ref, dy))):
        out[...] = jnp.dot(
            turned[k * hidden : (k + 1) * hidden, :], right, preferred_element_type=f32
        ).astype(bf16)


def weight_grads(coef_a, coef_b, rows_a, rows_b):
    rows, width = rows_a.shape[0], rows_a.shape[1] // 2
    hidden = coef_a.shape[1] // 3
    block = 512
    blocks = width // block
    whole = lambda i: (0, 0)
    x_at = pl.BlockSpec((rows, block), lambda i: (0, i))
    dy_at = pl.BlockSpec((rows, block), lambda i: (0, blocks + i))
    rows_a, rows_b = in_hbm(rows_a), in_hbm(rows_b)
    return pl.pallas_call(
        weight_kernel,
        grid=(blocks,),
        in_specs=[pl.BlockSpec(coef_a.shape, whole)] * 2 + [x_at, dy_at] * 2,
        out_specs=[pl.BlockSpec((hidden, block), lambda i: (0, i))] * 3,
        out_shape=[jax.ShapeDtypeStruct((hidden, width), bf16)] * 3,
        scratch_shapes=[pltpu.VMEM((3 * hidden, 2 * rows), bf16)],
        name="weight_grads",
        cost_estimate=pl.CostEstimate(
            flops=12 * rows * hidden * width,
            bytes_accessed=6 * hidden * width + 8 * rows * width,
            transcendentals=0,
        ),
        compiler_params=pltpu.CompilerParams(vmem_limit_bytes=65472 * 1024),
    )(coef_a, coef_b, rows_a, rows_a, rows_b, rows_b)


def combine_kernel(turned_ref, ret_ref, out_ref):
    out_ref[...] = jnp.dot(
        turned_ref[...], ret_ref[...], preferred_element_type=f32
    ).astype(bf16)


def combine(turned, ret):
    count, rows = turned.shape
    width = ret.shape[1]
    block = width // 4
    return pl.pallas_call(
        combine_kernel,
        grid=(width // block,),
        in_specs=[
            pl.BlockSpec((count, rows), lambda i: (0, 0)),
            pl.BlockSpec((rows, block), lambda i: (0, i)),
        ],
        out_specs=pl.BlockSpec((count, block), lambda i: (0, i)),
        out_shape=jax.ShapeDtypeStruct((count, width), bf16),
        name="combine",
        cost_estimate=pl.CostEstimate(
            flops=2 * rows * count * width, bytes_accessed=2 * (rows + count) * width, transcendentals=0
        ),
        compiler_params=pltpu.CompilerParams(vmem_limit_bytes=65472 * 1024),
    )(turned, ret)


def exchange(rows):
    return lax.all_to_all(rows, "ep", split_axis=0, concat_axis=0, tiled=True)


def swap(value):
    return lax.ppermute(value, "tp", [(0, 1), (1, 0)])


def local(tokens, expert_ids, gate_weights, grad_out, w_gate, w_up, w_down):
    experts = lax.axis_size("ep")
    own = (w_gate[0], w_up[0], w_down[0])
    send, match = gather(experts, expert_ids.T, gate_weights.T, tokens, grad_out)
    recv = exchange(send)
    partner = tuple(swap(w) for w in own)
    turned = match.T
    ret, coef, coef_sent = expert_terms(recv, own, partner)
    back = exchange(ret)
    coef_got, rows_got = swap(coef_sent), swap(recv)
    grads = weight_grads(coef, coef_got, recv, rows_got)
    grad_tokens = combine(turned, back)
    return (grad_tokens, *(g[None] for g in grads))


def solution(mesh):
    rows = P(("ep", "tp"), None)
    weight = P("ep", "tp", None)
    return jax.shard_map(
        local,
        mesh=mesh,
        in_specs=(rows, rows, rows, rows, weight, weight, weight),
        out_specs=(rows, weight, weight, weight),
        check_vma=False,
    )
```

time: 156 us -> 126 us (0.81)
  blocking collectives: 62.3 us -> 0 us
  Pallas kernels: 0 us -> 37.1 us
  waiting for transfers between devices: 35.3 us -> 72.3 us
  matrix products: 28.8 us -> 0 us
  between operations: 13.8 us -> 0.7 us
  other arithmetic: 7.04 us -> 0 us
  starting transfers between devices: 7.1 us -> 13.7 us
    all_to_all x2 -> x0, blocking collectives: 62.3 us -> none  [the longest x1 32.8 us: local(): lax.all_to_all(send_dy, 'ep', split_axis=0, concat_axis=0, tiled=True)]
    all_to_all x1 -> x2, waiting for transfers between devices: 15.9 us -> 72.3 us  [exchange(): return lax.all_to_all(rows, 'ep', split_axis=0, concat_axis=0, tiled=True)]
    pallas_call x0 -> x4, Pallas kernels: none -> 37.1 us  [the longest x1 18.6 us: expert_terms(): pl.pallas_call(expert_kernel, in_specs=[vmem] + [anywhere] * 6, out_specs...]
    dot_general x10 -> x0, matrix products: 28.8 us -> none  [the longest x1 4.52 us: expert_terms(): lax.dot_general(d_pre, rows_x, contract_first, preferred_element_type=jnp...]
    reduce_scatter x1 -> x0, waiting for transfers between devices: 13.5 us -> none  [local(): lax.psum_scatter(jnp.dot(fold_stored, joined, preferred_element_type=jnp....]
    all_to_all x1 -> x2, starting transfers between devices: 6.98 us -> 13 us  [exchange(): return lax.all_to_all(rows, 'ep', split_axis=0, concat_axis=0, tiled=True)]
    all_gather x2 -> x0, waiting for transfers between devices: 5.85 us -> none  [the longest x1 5.83 us: local(): lax.all_gather(recv_x, 'tp', axis=0, tiled=True)]
    reduce_sum x3 -> x0, other arithmetic: 3.3 us -> none  [the longest x1 1.71 us: local(): jnp.sum(jnp.where(match, gate_weights[None, :, :], 0.0), axis=(1, 2))]
  transfers between devices with their start and end apart: 4 -> 7, of which waited for: 3 -> 2; matrix products, arithmetic and copies ran while one was open for 10% -> 1% of each run, Pallas kernels for 0% -> 18%
where the time goes in v3:
time: 126 us; the launch traced here: 125 us
  waiting for transfers between devices  72.3 us (57%)
  Pallas kernels  37.1 us (29%)
  starting transfers between devices  13.7 us (11%)
  local copies, waits for them, and re-layouts  1.46 us (1%)
    all_to_all x2, waiting for transfers between devices, exchange(): return lax.all_to_all(rows, 'ep', split_axis=0, concat_axis=0, tiled=True)  72.3 us
    pallas_call x1, Pallas kernels, expert_terms(): pl.pallas_call(expert_kernel, in_specs=[vmem] + [anywhere] * 6, out_specs...  18.6 us
    all_to_all x2, starting transfers between devices, exchange(): return lax.all_to_all(rows, 'ep', split_axis=0, concat_axis=0, tiled=True)  13 us
    pallas_call x1, Pallas kernels, weight_grads(): pl.pallas_call(weight_kernel, grid=(blocks,), in_specs=[pl.BlockSpec(coef...  9.83 us
    pallas_call x1, Pallas kernels, gather(): pl.pallas_call(functools.partial(gather_kernel, experts, half), grid=(2 *...  4.86 us
    pallas_call x1, Pallas kernels, combine(): pl.pallas_call(combine_kernel, grid=(width // block,), in_specs=[pl.Block...  3.76 us
  transfers between devices with their start and end apart: 7, of which 2 were waited for; matrix products, arithmetic and copies ran while one was open for 1% of the time, Pallas kernels for 18%

profile of v3, /device:TPU:8, one launch (start us, length us, event | category | flops | bytes accessed | tf_op | source)
XLA Modules:
  0.0 125.2 jit_solution(8981929463204998279)
XLA Ops:
  0.6 0.0 copy-start.1
  0.6 4.9 %gather.1 = (bf16[128,8192]{1,0:T(8,128)(2,1)}, bf16[128,128]{1,0:T(8,128)(2,1)S(1)}) custom-call(s32[8,128]{1,0:T(8,128)} %bitcast.22, f32[8,128]{1,0:T(8,128)} %bitcast.23, bf16[128,4096]{1,0:T(8,128)(2,1)} %tok_ref.1, bf16[128,4096]{1,0:T(8,128)(2,1)} %dy_ref.1), custom_call_target="tpu_custom_call" | custom-call | flops 268435456 | bytes 4194304 | tf_op jit(solution)/shard_map/gather/pallas_call | solution.py:79
  5.5 7.2 %all-to-all-start = ((bf16[16,8,8192]{2,1,0:T(8,128)(2,1)}), bf16[16,8,8192]{2,1,0:T(8,128)(2,1)}, u32[]{:S(2)}, u32[]{:S(2)}) async-start(bf16[16,8,8192]{2,1,0:T(8,128)(2,1)} %bitcast.19), calls=%async_computation | async-start | bytes 4194304 | tf_op jit(solution)/shard_map/all_to_all | solution.py:286
  12.7 0.0 copy-done.1
  12.7 0.1 collective-permute-start
  12.8 0.5 collective-permute-start.1
  13.3 0.1 collective-permute-start.2
  13.4 46.7 %all-to-all-done = bf16[16,8,8192]{2,1,0:T(8,128)(2,1)} async-done(((bf16[16,8,8192]{2,1,0:T(8,128)(2,1)}), bf16[16,8,8192]{2,1,0:T(8,128)(2,1)}, u32[]{:S(2)}, u32[]{:S(2)}) %all-to-all-start) | async-done | bytes 2097184 | tf_op jit(solution)/shard_map/all_to_all | solution.py:286
  60.1 0.0 collective-permute-start.4
  60.1 0.0 collective-permute-done.gate_b
  60.1 0.0 collective-permute-done.1.up_b
  60.1 0.0 collective-permute-done.2.down_b
  60.1 18.6 %expert_terms.1 = (bf16[128,4096]{1,0:T(8,128)(2,1)}, bf16[128,1152]{1,0:T(8,128)(2,1)S(1)}, bf16[128,1152]{1,0:T(8,128)(2,1)}) custom-call(bf16[128,8192]{1,0:T(8,128)(2,1)} %bitcast.4.recv_ref.x_a.dy_a, bf16[384,4096]{1,0:T(8,128)(2,1)} %bitcast.13, bf16[384,4096]{1,0:T(8,128)(2,1)} %bitcast.16, bf16[384,4096]{1,0:T(8,128)(2,1)} %bitcast.18, ...), custom_call_target="tpu_custom_call" | custom-call | flops 4026531840 | bytes 22020096 | tf_op jit(solution)/shard_map/expert_terms/pallas_call | solution.py:190
  78.7 0.0 copy-start
  78.7 0.7 copy-done
  79.5 5.8 %all-to-all-start.1 = ((bf16[16,8,4096]{2,1,0:T(8,128)(2,1)}), bf16[16,8,4096]{2,1,0:T(8,128)(2,1)}, u32[]{:S(2)}, u32[]{:S(2)}) async-start(bf16[16,8,4096]{2,1,0:T(8,128)(2,1)} %bitcast.20), calls=%async_computation.1 | async-start | bytes 2097152 | tf_op jit(solution)/shard_map/all_to_all | solution.py:286
  85.3 0.0 collective-permute-start.3
  85.3 0.7 copy.11
  86.0 25.6 %all-to-all-done.1 = bf16[16,8,4096]{2,1,0:T(8,128)(2,1)} async-done(((bf16[16,8,4096]{2,1,0:T(8,128)(2,1)}), bf16[16,8,4096]{2,1,0:T(8,128)(2,1)}, u32[]{:S(2)}, u32[]{:S(2)}) %all-to-all-start.1) | async-done | bytes 1048608 | tf_op jit(solution)/shard_map/all_to_all | solution.py:286
  111.6 3.8 %combine.1 = bf16[128,4096]{1,0:T(8,128)(2,1)} custom-call(bf16[128,128]{1,0:T(8,128)(2,1)} %bitcast.21, bf16[128,4096]{1,0:T(8,128)(2,1)} %bitcast.9.ret_ref), custom_call_target="tpu_custom_call" | custom-call | flops 134217728 | bytes 2097152 | tf_op jit(solution)/shard_map/combine/pallas_call | solution.py:268
  115.4 0.0 collective-permute-done.3.coef_b
  115.4 0.0 collective-permute-done.4.x_b.dy_b
  115.4 9.8 %weight_grads.1 = (bf16[384,4096]{1,0:T(8,128)(2,1)}, bf16[384,4096]{1,0:T(8,128)(2,1)}, bf16[384,4096]{1,0:T(8,128)(2,1)}) custom-call(bf16[128,1152]{1,0:T(8,128)(2,1)} %copy-done, bf16[128,1152]{1,0:T(8,128)(2,1)} %collective-permute-done.3.coef_b, bf16[128,8192]{1,0:T(8,128)(2,1)} %bitcast.4.recv_ref.x_a.dy_a, ...), custom_call_target="tpu_custom_call" | custom-call | flops 2415919104 | bytes 13631488 | tf_op jit(solution)/shard_map/weight_grads/pallas_call | solution.py:241
Async XLA Ops:
  0.6 12.1 %copy-start.1 = (bf16[1,384,4096]{2,1,0:T(8,128)(2,1)S(1)}, bf16[1,384,4096]{2,1,0:T(8,128)(2,1)}, u32[]{:S(2)}) copy-start(bf16[1,384,4096]{2,1,0:T(8,128)(2,1)} %param.11) | copy-start | bytes 9437188
  5.5 54.6 %all-to-all-start = ((bf16[16,8,8192]{2,1,0:T(8,128)(2,1)}), bf16[16,8,8192]{2,1,0:T(8,128)(2,1)}, u32[]{:S(2)}, u32[]{:S(2)}) async-start(bf16[16,8,8192]{2,1,0:T(8,128)(2,1)} %bitcast.19), calls=%async_computation | async-start | bytes 4194304 | tf_op jit(solution)/shard_map/all_to_all | solution.py:286
  12.7 47.3 %collective-permute-start = (bf16[384,4096]{1,0:T(8,128)(2,1)S(1)}, bf16[384,4096]{1,0:T(8,128)(2,1)}, u32[]{:S(2)}, u32[]{:S(2)}) collective-permute-start(bf16[384,4096]{1,0:T(8,128)(2,1)S(1)} %bitcast.14), channel_id=1, source_target_pairs={{0,1},{1,0},{2,3},{3,2},{4,5},{5,4},{6,7},{7,6},{8,9},{9,8},{10,11... | collective-permute-start | bytes 9437192 | tf_op jit(solution)/shard_map/ppermute | solution.py:290
  12.8 47.3 %collective-permute-start.1 = (bf16[384,4096]{1,0:T(8,128)(2,1)}, bf16[384,4096]{1,0:T(8,128)(2,1)}, u32[]{:S(2)}, u32[]{:S(2)}) collective-permute-start(bf16[384,4096]{1,0:T(8,128)(2,1)} %bitcast.15), channel_id=1, source_target_pairs={{0,1},{1,0},{2,3},{3,2},{4,5},{5,4},{6,7},{7,6},{8,9},{9,8},{10,11... | collective-permute-start | bytes 9437192 | tf_op jit(solution)/shard_map/ppermute | solution.py:290
  13.3 46.8 %collective-permute-start.2 = (bf16[384,4096]{1,0:T(8,128)(2,1)}, bf16[384,4096]{1,0:T(8,128)(2,1)}, u32[]{:S(2)}, u32[]{:S(2)}) collective-permute-start(bf16[384,4096]{1,0:T(8,128)(2,1)} %bitcast.17), channel_id=1, source_target_pairs={{0,1},{1,0},{2,3},{3,2},{4,5},{5,4},{6,7},{7,6},{8,9},{9,8},{10,11... | collective-permute-start | bytes 9437192 | tf_op jit(solution)/shard_map/ppermute | solution.py:290
  60.1 55.3 %collective-permute-start.4 = (bf16[128,8192]{1,0:T(8,128)(2,1)}, bf16[128,8192]{1,0:T(8,128)(2,1)}, u32[]{:S(2)}, u32[]{:S(2)}) collective-permute-start(bf16[128,8192]{1,0:T(8,128)(2,1)} %bitcast.4.recv_ref.x_a.dy_a), channel_id=1, source_target_pairs={{0,1},{1,0},{2,3},{3,2},{4,5},{5,4},{6,7},{7,6},{8,9},{9,8},{10,11... | collective-permute-start | bytes 6291464 | tf_op jit(solution)/shard_map/ppermute | solution.py:290
  78.7 0.7 copy-start
  79.5 32.1 %all-to-all-start.1 = ((bf16[16,8,4096]{2,1,0:T(8,128)(2,1)}), bf16[16,8,4096]{2,1,0:T(8,128)(2,1)}, u32[]{:S(2)}, u32[]{:S(2)}) async-start(bf16[16,8,4096]{2,1,0:T(8,128)(2,1)} %bitcast.20), calls=%async_computation.1 | async-start | bytes 2097152 | tf_op jit(solution)/shard_map/all_to_all | solution.py:286
  85.3 30.1 %collective-permute-start.3 = (bf16[128,1152]{1,0:T(8,128)(2,1)}, bf16[128,1152]{1,0:T(8,128)(2,1)}, u32[]{:S(2)}, u32[]{:S(2)}) collective-permute-start(bf16[128,1152]{1,0:T(8,128)(2,1)} %get-tuple-element.16), channel_id=1, source_target_pairs={{0,1},{1,0},{2,3},{3,2},{4,5},{5,4},{6,7},{7,6},{8,9},{9,8},{10,11... | collective-permute-start | bytes 884744 | tf_op jit(solution)/shard_map/ppermute | solution.py:290

commit v4 on v3

v4 whole, which is shorter than its diff:
```python
import functools

import jax
import jax.numpy as jnp
from jax import lax
from jax.experimental import pallas as pl
from jax.experimental.pallas import tpu as pltpu
from jax.sharding import PartitionSpec as P


CAP = 8
MIB = 1 << 20

f32 = jnp.float32
bf16 = jnp.bfloat16


def in_hbm(x):
    return pltpu.with_memory_space_constraint(x, pltpu.HBM)


def in_vmem(x):
    return pltpu.with_memory_space_constraint(x, pltpu.VMEM)


def route(experts, ids_ref, gates_ref, match_ref, gate_s):
    rows, count = match_ref.shape
    expert_at = lax.broadcasted_iota(jnp.int32, (experts, count), 0)
    member = jnp.zeros((experts, count), f32)
    for k in range(ids_ref.shape[0]):
        member += jnp.where(ids_ref[k : k + 1, :] == expert_at, 1.0, 0.0)
    earlier = jnp.where(
        lax.broadcasted_iota(jnp.int32, (count, count), 0)
        < lax.broadcasted_iota(jnp.int32, (count, count), 1),
        1.0,
        0.0,
    ).astype(bf16)
    before = jnp.dot(member.astype(bf16), earlier, preferred_element_type=f32)
    row = lax.broadcasted_iota(jnp.int32, (rows, count), 0)
    match = jnp.zeros((rows, count), f32)
    gate = jnp.zeros((rows, count), f32)
    for k in range(ids_ref.shape[0]):
        named = ids_ref[k : k + 1, :]
        place = jnp.sum(
            jnp.where(named == expert_at, before, 0.0), axis=0, keepdims=True
        ).astype(jnp.int32)
        hit = jnp.where(named < experts, named * CAP + place, -1) == row
        match = jnp.where(hit, 1.0, match)
        gate = jnp.where(hit, gates_ref[k : k + 1, :], gate)
    match_ref[...] = match.astype(bf16)
    gate_s[...] = jnp.broadcast_to(jnp.sum(gate, axis=1, keepdims=True), gate_s.shape)


def gather_kernel(
    experts, ids_ref, gates_ref, tok_ref, dy_ref, send_ref, match_ref,
    ids_s, gates_s, rows_s, match_s, gate_s, out_s, sems, out_sems,
):
    blocks, _, block = rows_s.shape
    half = blocks // 2
    small = [
        pltpu.make_async_copy(ids_ref, ids_s, sems.at[blocks]),
        pltpu.make_async_copy(gates_ref, gates_s, sems.at[blocks + 1]),
    ]

    def load(i):
        src = tok_ref if i < half else dy_ref
        cols = pl.ds(i % half * block, block)
        return pltpu.make_async_copy(src.at[:, cols], rows_s.at[i], sems.at[i])

    def store(i):
        cols = pl.ds(i * block, block)
        return pltpu.make_async_copy(out_s.at[i], send_ref.at[:, cols], out_sems.at[i])

    for copy in small:
        copy.start()
    for i in range(blocks):
        load(i).start()
    for copy in small:
        copy.wait()
    route(experts, ids_s, gates_s, match_s, gate_s)
    keep = pltpu.make_async_copy(match_s, match_ref, out_sems.at[blocks])
    for i in range(blocks):
        load(i).wait()
        picked = jnp.dot(match_s[...], rows_s[i], preferred_element_type=f32)
        if i >= half:
            picked = gate_s[:, :1] * picked
        out_s[i] = picked.astype(bf16)
        store(i).start()
    keep.start()
    for i in range(blocks):
        store(i).wait()
    keep.wait()


def gather(experts, ids, gates, tokens, grad_out):
    count, width = tokens.shape
    rows = experts * CAP
    blocks = 8
    block = 2 * width // blocks
    anywhere = pl.BlockSpec(memory_space=pl.ANY)
    return pl.pallas_call(
        functools.partial(gather_kernel, experts),
        in_specs=[anywhere] * 4,
        out_specs=[anywhere] * 2,
        out_shape=[pltpu.HBM((rows, 2 * width), bf16), pltpu.HBM((rows, count), bf16)],
        scratch_shapes=[
            pltpu.VMEM(ids.shape, ids.dtype),
            pltpu.VMEM(gates.shape, gates.dtype),
            pltpu.VMEM((blocks, count, block), bf16),
            pltpu.VMEM((rows, count), bf16),
            pltpu.VMEM((rows, 128), f32),
            pltpu.VMEM((blocks, rows, block), bf16),
            pltpu.SemaphoreType.DMA((blocks + 2,)),
            pltpu.SemaphoreType.DMA((blocks + 1,)),
        ],
        name="gather",
        cost_estimate=pl.CostEstimate(
            flops=4 * rows * count * width, bytes_accessed=4 * width * (rows + count), transcendentals=0
        ),
        compiler_params=pltpu.CompilerParams(
            vmem_limit_bytes=8 * MIB + 8 * width * (rows + count)
        ),
    )(in_hbm(ids), in_hbm(gates), in_hbm(tokens), in_hbm(grad_out))


def expert_kernel(
    recv_ref, gate_a, up_a, down_a, gate_b, up_b, down_b, ret_ref, own_ref, partner_ref,
    joined_s, down_s, pre_s, dact_s, fold_s, total_s, coef_s, out_s, sems, coef_sems, out_sems,
):
    blocks, _, block = joined_s.shape
    hidden = gate_a.shape[0]
    width = blocks * block
    halves = ((gate_a, up_a, down_a), (gate_b, up_b, down_b))

    def loads(h, i):
        cols = pl.ds(i * block, block)
        dsts = (
            joined_s.at[i, pl.ds(2 * h * hidden, hidden)],
            joined_s.at[i, pl.ds((2 * h + 1) * hidden, hidden)],
            down_s.at[i, pl.ds(h * hidden, hidden)],
        )
        return [
            pltpu.make_async_copy(ref.at[:, cols], dst, sems.at[h, i, k])
            for k, (ref, dst) in enumerate(zip(halves[h], dsts))
        ]

    def store(i):
        return pltpu.make_async_copy(
            out_s.at[i], ret_ref.at[:, pl.ds(i * block, block)], out_sems.at[i]
        )

    for h in range(2):
        for i in range(blocks):
            for copy in loads(h, i):
                copy.start()

    contract_last = (((1,), (1,)), ((), ()))
    kept = []
    for h, coef_ref in enumerate((own_ref, partner_ref)):
        for i in range(blocks):
            for copy in loads(h, i):
                copy.wait()
            x = recv_ref[:, i * block : (i + 1) * block]
            dy = recv_ref[:, width + i * block : width + (i + 1) * block]
            pre = lax.dot_general(
                joined_s[i, 2 * h * hidden : 2 * (h + 1) * hidden],
                x,
                contract_last,
                preferred_element_type=f32,
            )
            dact = lax.dot_general(
                down_s[i, h * hidden : (h + 1) * hidden],
                dy,
                contract_last,
                preferred_element_type=f32,
            )
            pre_s[...] = pre if i == 0 else pre_s[...] + pre
            dact_s[...] = dact if i == 0 else dact_s[...] + dact

        step = 32

        @pl.loop(0, hidden // step)
        def _(b):
            at = pl.multiple_of(b * step, step)
            g = pre_s[pl.ds(at, step), :]
            u = pre_s[pl.ds(hidden + at, step), :]
            a = dact_s[pl.ds(at, step), :]
            s = jax.nn.sigmoid(g)
            d_pre = (a * u * s * (1.0 + g * (1.0 - s))).astype(bf16)
            d_up = (a * g * s).astype(bf16)
            coef_s[h, pl.ds(at, step), :] = d_pre
            coef_s[h, pl.ds(hidden + at, step), :] = d_up
            coef_s[h, pl.ds(2 * hidden + at, step), :] = (g * s * u).astype(bf16)

        kept.append(pltpu.make_async_copy(coef_s.at[h], coef_ref, coef_sems.at[h]))
        kept[h].start()
        fold_s[...] = coef_s[h, : 2 * hidden, :].T
        for i in range(blocks):
            part = jnp.dot(
                fold_s[...],
                joined_s[i, 2 * h * hidden : 2 * (h + 1) * hidden],
                preferred_element_type=f32,
            )
            if h == 0:
                total_s[i] = part
            else:
                out_s[i] = (total_s[i] + part).astype(bf16)
                store(i).start()
    for i in range(blocks):
        store(i).wait()
    for copy in kept:
        copy.wait()


def expert_terms(recv, own, partner):
    rows, width = recv.shape[0], recv.shape[1] // 2
    hidden = own[0].shape[0]
    blocks = 4
    block = width // blocks
    anywhere = pl.BlockSpec(memory_space=pl.ANY)
    vmem = pl.BlockSpec(memory_space=pltpu.VMEM)
    coef = pltpu.HBM((3 * hidden, rows), bf16)
    return pl.pallas_call(
        expert_kernel,
        in_specs=[vmem] + [anywhere] * 6,
        out_specs=[anywhere] * 3,
        out_shape=[pltpu.HBM((rows, width), bf16), coef, coef],
        scratch_shapes=[
            pltpu.VMEM((blocks, 4 * hidden, block), bf16),
            pltpu.VMEM((blocks, 2 * hidden, block), bf16),
            pltpu.VMEM((2 * hidden, rows), f32),
            pltpu.VMEM((hidden, rows), f32),
            pltpu.VMEM((rows, 2 * hidden), bf16),
            pltpu.VMEM((blocks, rows, block), f32),
            pltpu.VMEM((2, 3 * hidden, rows), bf16),
            pltpu.VMEM((blocks, rows, block), bf16),
            pltpu.SemaphoreType.DMA((2, blocks, 3)),
            pltpu.SemaphoreType.DMA((2,)),
            pltpu.SemaphoreType.DMA((blocks,)),
        ],
        name="expert_terms",
        cost_estimate=pl.CostEstimate(
            flops=20 * rows * hidden * width,
            bytes_accessed=12 * hidden * width + 6 * rows * width,
            transcendentals=2 * rows * hidden,
        ),
        compiler_params=pltpu.CompilerParams(
            vmem_limit_bytes=8 * MIB + 12 * hidden * width + 8 * rows * width + 40 * rows * hidden
        ),
    )(in_vmem(recv), *(in_hbm(w) for w in (*own, *partner)))


def weight_kernel(coef_a, coef_b, x_a, dy_a, x_b, dy_b, gate_ref, up_ref, down_ref):
    hidden = gate_ref.shape[0]
    x = jnp.concatenate([x_a[...], x_b[...]], axis=0)
    dy = jnp.concatenate([dy_a[...], dy_b[...]], axis=0)
    for k, (out, right) in enumerate(((gate_ref, x), (up_ref, x), (down_ref, dy))):
        at = slice(k * hidden, (k + 1) * hidden)
        left = jnp.concatenate([coef_a[at, :], coef_b[at, :]], axis=1)
        out[...] = jnp.dot(left, right, preferred_element_type=f32).astype(bf16)


def weight_grads(coef_a, coef_b, rows_a, rows_b):
    rows, width = rows_a.shape[0], rows_a.shape[1] // 2
    hidden = coef_a.shape[0] // 3
    block = 512
    blocks = width // block
    whole = lambda i: (0, 0)
    x_at = pl.BlockSpec((rows, block), lambda i: (0, i))
    dy_at = pl.BlockSpec((rows, block), lambda i: (0, blocks + i))
    rows_a, rows_b = in_hbm(rows_a), in_hbm(rows_b)
    return pl.pallas_call(
        weight_kernel,
        grid=(blocks,),
        in_specs=[pl.BlockSpec(coef_a.shape, whole)] * 2 + [x_at, dy_at] * 2,
        out_specs=[pl.BlockSpec((hidden, block), lambda i: (0, i))] * 3,
        out_shape=[jax.ShapeDtypeStruct((hidden, width), bf16)] * 3,
        name="weight_grads",
        cost_estimate=pl.CostEstimate(
            flops=12 * rows * hidden * width,
            bytes_accessed=6 * hidden * width + 8 * rows * width,
            transcendentals=0,
        ),
        compiler_params=pltpu.CompilerParams(vmem_limit_bytes=65472 * 1024),
    )(in_hbm(coef_a), in_hbm(coef_b), rows_a, rows_a, rows_b, rows_b)


def combine_kernel(turned_ref, ret_ref, out_ref, turned_s, ret_s, out_s, sems, out_sems):
    blocks, _, block = ret_s.shape

    def load(i):
        cols = pl.ds(i * block, block)
        return pltpu.make_async_copy(ret_ref.at[:, cols], ret_s.at[i], sems.at[i])

    def store(i):
        cols = pl.ds(i * block, block)
        return pltpu.make_async_copy(out_s.at[i], out_ref.at[:, cols], out_sems.at[i])

    first = pltpu.make_async_copy(turned_ref, turned_s, sems.at[blocks])
    first.start()
    for i in range(blocks):
        load(i).start()
    first.wait()
    for i in range(blocks):
        load(i).wait()
        out_s[i] = jnp.dot(turned_s[...], ret_s[i], preferred_element_type=f32).astype(bf16)
        store(i).start()
    for i in range(blocks):
        store(i).wait()


def combine(turned, ret):
    count, rows = turned.shape
    width = ret.shape[1]
    blocks = 4
    block = width // blocks
    anywhere = pl.BlockSpec(memory_space=pl.ANY)
    return pl.pallas_call(
        combine_kernel,
        in_specs=[anywhere] * 2,
        out_specs=anywhere,
        out_shape=pltpu.HBM((count, width), bf16),
        scratch_shapes=[
            pltpu.VMEM((count, rows), bf16),
            pltpu.VMEM((blocks, rows, block), bf16),
            pltpu.VMEM((blocks, count, block), bf16),
            pltpu.SemaphoreType.DMA((blocks + 1,)),
            pltpu.SemaphoreType.DMA((blocks,)),
        ],
        name="combine",
        cost_estimate=pl.CostEstimate(
            flops=2 * rows * count * width, bytes_accessed=2 * (rows + count) * width, transcendentals=0
        ),
        compiler_params=pltpu.CompilerParams(
            vmem_limit_bytes=8 * MIB + 4 * (rows + count) * width
        ),
    )(in_hbm(turned), in_hbm(ret))


def exchange(rows):
    return lax.all_to_all(rows, "ep", split_axis=0, concat_axis=0, tiled=True)


def swap(value):
    return lax.ppermute(value, "tp", [(0, 1), (1, 0)])


def local(tokens, expert_ids, gate_weights, grad_out, w_gate, w_up, w_down):
    experts = lax.axis_size("ep")
    own = (w_gate[0], w_up[0], w_down[0])
    send, match = gather(experts, expert_ids.T, gate_weights.T, tokens, grad_out)
    recv = exchange(send)
    partner = tuple(swap(w) for w in own)
    turned = match.T
    ret, coef, coef_sent = expert_terms(recv, own, partner)
    back = exchange(ret)
    coef_got, rows_got = swap(coef_sent), swap(recv)
    grads = weight_grads(coef, coef_got, recv, rows_got)
    grad_tokens = combine(turned, back)
    return (grad_tokens, *(g[None] for g in grads))


def solution(mesh):
    rows = P(("ep", "tp"), None)
    weight = P("ep", "tp", None)
    return jax.shard_map(
        local,
        mesh=mesh,
        in_specs=(rows, rows, rows, rows, weight, weight, weight),
        out_specs=(rows, weight, weight, weight),
        check_vma=False,
    )
```

time: 126 us -> 119 us (0.944)
  Pallas kernels: 37.1 us -> 30.2 us
    pallas_call x1, Pallas kernels: 18.6 us -> 14.4 us  [expert_terms(): pl.pallas_call(expert_kernel, in_specs=[vmem] + [anywhere] * 6, out_specs...]
    pallas_call x2, Pallas kernels: 8.62 us -> 6.23 us  [the longest x1 3.61 us: gather(): pl.pallas_call(functools.partial(gather_kernel, experts), in_specs=[anywh...]
  transfers between devices with their start and end apart: 7 -> 7, of which waited for: 2 -> 2; matrix products, arithmetic and copies ran while one was open for 1% -> 1% of each run, Pallas kernels for 18% -> 14%
where the time goes in v4:
time: 119 us; the launch traced here: 118 us
  waiting for transfers between devices  71.4 us (60%)
  Pallas kernels  30.2 us (25%)
  starting transfers between devices  13.6 us (11%)
  local copies, waits for them, and re-layouts  2.38 us (2%)
    all_to_all x2, waiting for transfers between devices, exchange(): return lax.all_to_all(rows, 'ep', split_axis=0, concat_axis=0, tiled=True)  71.4 us
    pallas_call x1, Pallas kernels, expert_terms(): pl.pallas_call(expert_kernel, in_specs=[vmem] + [anywhere] * 6, out_specs...  14.4 us
    all_to_all x2, starting transfers between devices, exchange(): return lax.all_to_all(rows, 'ep', split_axis=0, concat_axis=0, tiled=True)  13.1 us
    pallas_call x1, Pallas kernels, weight_grads(): pl.pallas_call(weight_kernel, grid=(blocks,), in_specs=[pl.BlockSpec(coef...  9.6 us
    pallas_call x1, Pallas kernels, gather(): pl.pallas_call(functools.partial(gather_kernel, experts), in_specs=[anywh...  3.61 us
    pallas_call x1, Pallas kernels, combine(): pl.pallas_call(combine_kernel, in_specs=[anywhere] * 2, out_specs=anywher...  2.62 us
  transfers between devices with their start and end apart: 7, of which 2 were waited for; matrix products, arithmetic and copies ran while one was open for 1% of the time, Pallas kernels for 14%

profile of v4, /device:TPU:8, one launch (start us, length us, event | category | flops | bytes accessed | tf_op | source)
XLA Modules:
  0.0 118.4 jit_solution(16917266304478943892)
XLA Ops:
  0.6 3.6 %gather.1 = (bf16[128,8192]{1,0:T(8,128)(2,1)}, bf16[128,128]{1,0:T(8,128)(2,1)}) custom-call(s32[8,128]{1,0:T(8,128)} %bitcast.27, f32[8,128]{1,0:T(8,128)} %bitcast.28, bf16[128,4096]{1,0:T(8,128)(2,1)} %tok_ref.1, bf16[128,4096]{1,0:T(8,128)(2,1)} %dy_ref.1), custom_call_target="tpu_custom_call" | custom-call | flops 268435456 | bytes 4194304 | tf_op jit(solution)/shard_map/gather/pallas_call | solution.py:101
  4.3 7.2 %all-to-all-start = ((bf16[16,8,8192]{2,1,0:T(8,128)(2,1)}), bf16[16,8,8192]{2,1,0:T(8,128)(2,1)S(1)}, u32[]{:S(2)}, u32[]{:S(2)}) async-start(bf16[16,8,8192]{2,1,0:T(8,128)(2,1)} %bitcast.24), calls=%async_computation | async-start | bytes 4194304 | tf_op jit(solution)/shard_map/all_to_all | solution.py:341
  11.5 0.0 collective-permute-start
  11.5 0.5 collective-permute-start.1
  12.0 0.1 collective-permute-start.2
  12.1 46.6 %all-to-all-done = bf16[16,8,8192]{2,1,0:T(8,128)(2,1)S(1)} async-done(((bf16[16,8,8192]{2,1,0:T(8,128)(2,1)}), bf16[16,8,8192]{2,1,0:T(8,128)(2,1)S(1)}, u32[]{:S(2)}, u32[]{:S(2)}) %all-to-all-start) | async-done | bytes 2097184 | tf_op jit(solution)/shard_map/all_to_all | solution.py:341
  58.7 0.0 copy-start
  58.7 0.0 copy-start.3
  58.7 0.0 collective-permute-start.4
  58.7 0.0 collective-permute-done.gate_b
  58.7 0.0 collective-permute-done.1.up_b
  58.7 0.0 collective-permute-done.2.down_b
  58.8 14.4 %expert_terms.1 = (bf16[128,4096]{1,0:T(8,128)(2,1)}, bf16[1152,128]{1,0:T(8,128)(2,1)}, bf16[1152,128]{1,0:T(8,128)(2,1)}) custom-call(bf16[128,8192]{1,0:T(8,128)(2,1)S(1)} %bitcast.14, bf16[384,4096]{1,0:T(8,128)(2,1)} %bitcast.19, bf16[384,4096]{1,0:T(8,128)(2,1)} %bitcast.21, bf16[384,4096]{1,0:T(8,128)(2,1)} %bitcast.23, ...), custom_call_target="tpu_custom_call" | custom-call | flops 4026531840 | bytes 22020096 | tf_op jit(solution)/shard_map/expert_terms/pallas_call | solution.py:223
  73.2 0.0 copy-done
  73.2 5.8 %all-to-all-start.1 = ((bf16[16,8,4096]{2,1,0:T(8,128)(2,1)}), bf16[16,8,4096]{2,1,0:T(8,128)(2,1)S(1)}, u32[]{:S(2)}, u32[]{:S(2)}) async-start(bf16[16,8,4096]{2,1,0:T(8,128)(2,1)} %bitcast.25), calls=%async_computation.1 | async-start | bytes 2097152 | tf_op jit(solution)/shard_map/all_to_all | solution.py:341
  79.0 0.0 collective-permute-start.3
  79.0 0.0 copy-done.3
  79.0 0.7 copy.11
  79.7 24.7 %all-to-all-done.1 = bf16[16,8,4096]{2,1,0:T(8,128)(2,1)S(1)} async-done(((bf16[16,8,4096]{2,1,0:T(8,128)(2,1)}), bf16[16,8,4096]{2,1,0:T(8,128)(2,1)S(1)}, u32[]{:S(2)}, u32[]{:S(2)}) %all-to-all-start.1) | async-done | bytes 1048608 | tf_op jit(solution)/shard_map/all_to_all | solution.py:341
  104.5 0.0 copy-start.1
  104.5 1.0 copy-done.1
  105.4 2.6 %combine.1 = bf16[128,4096]{1,0:T(8,128)(2,1)} custom-call(bf16[128,128]{1,0:T(8,128)(2,1)} %bitcast.26, bf16[128,4096]{1,0:T(8,128)(2,1)} %bitcast.17), custom_call_target="tpu_custom_call" | custom-call | flops 134217728 | bytes 2097152 | tf_op jit(solution)/shard_map/combine/pallas_call | solution.py:318
  108.1 0.0 collective-permute-done.3.coef_b
  108.1 0.0 copy-start.2
  108.1 0.0 collective-permute-done.4.x_b.dy_b
  108.1 0.7 copy-done.2
  108.8 9.6 %weight_grads.1 = (bf16[384,4096]{1,0:T(8,128)(2,1)}, bf16[384,4096]{1,0:T(8,128)(2,1)}, bf16[384,4096]{1,0:T(8,128)(2,1)}) custom-call(bf16[1152,128]{1,0:T(8,128)(2,1)} %get-tuple-element.15.coef_a, bf16[1152,128]{1,0:T(8,128)(2,1)} %copy-done.2, bf16[128,8192]{1,0:T(8,128)(2,1)} %bitcast.15, bf16[128,8192]{1,0:T(8,128)(2,1)} %bitcast.16, ...), custom_call_target="tpu_custom_call" | custom-call | flops 2415919104 | bytes 13631488 | tf_op jit(solution)/shard_map/weight_grads/pallas_call | solution.py:272
Async XLA Ops:
  4.3 54.5 %all-to-all-start = ((bf16[16,8,8192]{2,1,0:T(8,128)(2,1)}), bf16[16,8,8192]{2,1,0:T(8,128)(2,1)S(1)}, u32[]{:S(2)}, u32[]{:S(2)}) async-start(bf16[16,8,8192]{2,1,0:T(8,128)(2,1)} %bitcast.24), calls=%async_computation | async-start | bytes 4194304 | tf_op jit(solution)/shard_map/all_to_all | solution.py:341
  11.5 47.2 %collective-permute-start = (bf16[384,4096]{1,0:T(8,128)(2,1)}, bf16[384,4096]{1,0:T(8,128)(2,1)}, u32[]{:S(2)}, u32[]{:S(2)}) collective-permute-start(bf16[384,4096]{1,0:T(8,128)(2,1)} %bitcast.18), channel_id=1, source_target_pairs={{0,1},{1,0},{2,3},{3,2},{4,5},{5,4},{6,7},{7,6},{8,9},{9,8},{10,11... | collective-permute-start | bytes 9437192 | tf_op jit(solution)/shard_map/ppermute | solution.py:345
  11.5 47.2 %collective-permute-start.1 = (bf16[384,4096]{1,0:T(8,128)(2,1)}, bf16[384,4096]{1,0:T(8,128)(2,1)}, u32[]{:S(2)}, u32[]{:S(2)}) collective-permute-start(bf16[384,4096]{1,0:T(8,128)(2,1)} %bitcast.20), channel_id=1, source_target_pairs={{0,1},{1,0},{2,3},{3,2},{4,5},{5,4},{6,7},{7,6},{8,9},{9,8},{10,11... | collective-permute-start | bytes 9437192 | tf_op jit(solution)/shard_map/ppermute | solution.py:345
  12.0 46.8 %collective-permute-start.2 = (bf16[384,4096]{1,0:T(8,128)(2,1)}, bf16[384,4096]{1,0:T(8,128)(2,1)}, u32[]{:S(2)}, u32[]{:S(2)}) collective-permute-start(bf16[384,4096]{1,0:T(8,128)(2,1)} %bitcast.22), channel_id=1, source_target_pairs={{0,1},{1,0},{2,3},{3,2},{4,5},{5,4},{6,7},{7,6},{8,9},{9,8},{10,11... | collective-permute-start | bytes 9437192 | tf_op jit(solution)/shard_map/ppermute | solution.py:345
  58.7 14.5 %copy-start = (bf16[16,8,8192]{2,1,0:T(8,128)(2,1)}, bf16[16,8,8192]{2,1,0:T(8,128)(2,1)S(1)}, u32[]{:S(2)}) copy-start(bf16[16,8,8192]{2,1,0:T(8,128)(2,1)S(1)} %all-to-all-done) | copy-start | bytes 6291460
  58.7 20.3 %copy-start.3 = (bf16[128,128]{1,0:T(8,128)(2,1)S(1)}, bf16[128,128]{1,0:T(8,128)(2,1)}, u32[]{:S(2)}) copy-start(bf16[128,128]{1,0:T(8,128)(2,1)} %get-tuple-element.12) | copy-start | bytes 98308
  58.7 49.3 %collective-permute-start.4 = (bf16[128,8192]{1,0:T(8,128)(2,1)S(1)}, bf16[128,8192]{1,0:T(8,128)(2,1)}, u32[]{:S(2)}, u32[]{:S(2)}) collective-permute-start(bf16[128,8192]{1,0:T(8,128)(2,1)S(1)} %bitcast.13), channel_id=1, source_target_pairs={{0,1},{1,0},{2,3},{3,2},{4,5},{5,4},{6,7},{7,6},{8,9},{9,8},{10,11... | collective-permute-start | bytes 6291464 | tf_op jit(solution)/shard_map/ppermute | solution.py:345
  73.2 31.3 %all-to-all-start.1 = ((bf16[16,8,4096]{2,1,0:T(8,128)(2,1)}), bf16[16,8,4096]{2,1,0:T(8,128)(2,1)S(1)}, u32[]{:S(2)}, u32[]{:S(2)}) async-start(bf16[16,8,4096]{2,1,0:T(8,128)(2,1)} %bitcast.25), calls=%async_computation.1 | async-start | bytes 2097152 | tf_op jit(solution)/shard_map/all_to_all | solution.py:341
  79.0 29.0 %collective-permute-start.3 = (bf16[1152,128]{1,0:T(8,128)(2,1)}, bf16[1152,128]{1,0:T(8,128)(2,1)S(1)}, u32[]{:S(2)}, u32[]{:S(2)}) collective-permute-start(bf16[1152,128]{1,0:T(8,128)(2,1)} %get-tuple-element.16), channel_id=1, source_target_pairs={{0,1},{1,0},{2,3},{3,2},{4,5},{5,4},{6,7},{7,6},{8,9},{9,8},{10,11... | collective-permute-start | bytes 884744 | tf_op jit(solution)/shard_map/ppermute | solution.py:345
  104.5 1.0 copy-start.1
  108.1 0.7 copy-start.2
